TPU v7x, 128 devices: a whole 4x4x4 slice. The times are simulated.
128 devices in a mesh: dp: 8 (over y, x_lo), ctx: 16 (over z, x_hi, core).
Axes of the slice: x: 4 (x_hi: 2, x_lo: 2; x = x_hi * 2 + x_lo), y: 4, z: 4, core: 2. Of those that a mesh axis runs over, the one named last changes fastest.
Arguments:
- queries: bfloat16 [8, 16384, 768], P('dp', 'ctx'), may hold values from -6 to 6
- keys: bfloat16 [8, 16384, 768], P('dp', 'ctx'), may hold values from -6 to 6
- values: bfloat16 [8, 16384, 768], P('dp', 'ctx'), may hold values from -6 to 6
- offsets: int32 [16], replicated, may hold values from 0 to 15
- w_out: bfloat16 [768, 768], replicated, may hold values from -0.875 to 0.875
- grad_out: bfloat16 [8, 16384, 768], P('dp', 'ctx'), may hold values from -6 to 6
Outputs:
- output: bfloat16 [8, 16384, 768], P('dp', 'ctx')
- grad_queries: bfloat16 [8, 16384, 768], P('dp', 'ctx')
- grad_keys: bfloat16 [8, 16384, 768], P('dp', 'ctx')
- grad_values: bfloat16 [8, 16384, 768], P('dp', 'ctx')
- weight_grad: float32 [768, 768], replicated
All inputs are finite; a program needn't handle non-finite values.
Results may differ from a plain program's by a relative error of at most 0.012.
Values may be sent and summed in bfloat16 or wider, within the bound.
No kernel may reach another device: no remote copies, remote signals or barrier semaphores. Data moves between devices by JAX's collectives and lax.ppermute only.
A program may use at most 192 MiB of HBM per device.

v0:
```python
import jax
import jax.numpy as jnp
from jax import lax
from jax.sharding import PartitionSpec as P

HEADS = 16
SEG = 1024
RATE = 16


def contract_rows(left, right):
    return lax.dot_general(
        left, right, (((0,), (0,)), ((), ())), preferred_element_type=jnp.float32
    )


def contract_cols(left, right):
    return lax.dot_general(
        left, right, (((1,), (1,)), ((), ())), preferred_element_type=jnp.float32
    )


def pick_rows(source, offset):
    grouped = source.reshape((source.shape[0] // RATE, RATE) + source.shape[1:])
    return lax.dynamic_index_in_dim(grouped, offset, 1, keepdims=False)


def place_rows(picked, offset):
    chosen = jnp.arange(RATE, dtype=jnp.int32) == offset
    shaped = chosen.reshape((1, RATE) + (1,) * (picked.ndim - 1))
    spread = jnp.where(shaped, jnp.expand_dims(picked, 1), jnp.zeros((), picked.dtype))
    return spread.reshape((picked.shape[0] * RATE,) + picked.shape[1:])


def head_mask(offsets):
    return jnp.arange(RATE, dtype=jnp.int32)[:, None] == offsets[None, :]


def pick_all(source, offsets):
    grouped = source.reshape(source.shape[0] // RATE, RATE, HEADS, -1)
    picked = jnp.where(head_mask(offsets)[None, :, :, None], grouped, jnp.zeros((), source.dtype))
    return jnp.sum(picked, axis=1).reshape(source.shape[0] // RATE, -1)


def place_all(picked, offsets):
    spread = jnp.where(
        head_mask(offsets)[None, :, :, None],
        picked.reshape(picked.shape[0], 1, HEADS, -1),
        jnp.zeros((), picked.dtype),
    )
    return spread.reshape(picked.shape[0] * RATE, -1)


def segment_view(source):
    return source.reshape(source.shape[0] // SEG, SEG, source.shape[1])


def split_heads(source, count):
    return source.reshape(source.shape[0], count, -1).transpose(1, 0, 2)


def join_heads(source):
    return source.transpose(1, 0, 2).reshape(source.shape[1], -1)


def near_scores_of(head_query, head_key):
    inv_root = head_query.shape[1] ** (-0.5)
    return (
        jnp.einsum(
            "gid,gjd->gij",
            segment_view(head_query),
            segment_view(head_key),
            preferred_element_type=jnp.float32,
        )
        * inv_root
    )


def far_section(sel_query, far_keys, far_values, near_sel):
    inv_root = sel_query.shape[1] ** (-0.5)
    far_scores = contract_cols(sel_query, far_keys) * inv_root
    joint_sel = jnp.logaddexp(near_sel, jax.nn.logsumexp(far_scores, axis=-1))
    far_prob = jnp.exp(far_scores - joint_sel[:, None]).astype(jnp.bfloat16)
    return (jnp.dot(far_prob, far_values, preferred_element_type=jnp.float32), joint_sel)


def merge_joint(near_lse, joint_sel, offset):
    chosen = (jnp.arange(RATE, dtype=jnp.int32) == offset)[None, :]
    return jnp.where(chosen, joint_sel[:, None], near_lse.reshape(-1, RATE)).reshape(-1)


def near_output(near_scores, head_value, joint_lse):
    near_prob = jnp.exp(near_scores - joint_lse.reshape(-1, SEG)[:, :, None]).astype(jnp.bfloat16)
    summed = jnp.einsum(
        "gij,gjd->gid", near_prob, segment_view(head_value), preferred_element_type=jnp.float32
    )
    return summed.reshape(joint_lse.shape[0], -1)


def forward_head(head_query, head_key, head_value, far_keys, far_values, offset):
    near_scores = near_scores_of(head_query, head_key)
    near_lse = jax.nn.logsumexp(near_scores, axis=-1).reshape(-1)
    far_out, joint_sel = far_section(
        pick_rows(head_query, offset), far_keys, far_values, pick_rows(near_lse, offset)
    )
    joint_lse = merge_joint(near_lse, joint_sel, offset)
    summed = near_output(near_scores, head_value, joint_lse) + place_rows(far_out, offset)
    return (summed.astype(jnp.bfloat16), joint_lse)


def near_grads(head_query, head_key, head_value, joint_lse, head_grad, inner_dot):
    inv_root = head_query.shape[1] ** (-0.5)
    row_count = head_query.shape[0]
    query_view = segment_view(head_query)
    key_view = segment_view(head_key)
    value_view = segment_view(head_value)
    grad_view = segment_view(head_grad)
    near_scores = (
        jnp.einsum("gid,gjd->gij", query_view, key_view, preferred_element_type=jnp.float32)
        * inv_root
    )
    near_prob = jnp.exp(near_scores - joint_lse.reshape(-1, SEG)[:, :, None])
    dprob = jnp.einsum("gid,gjd->gij", grad_view, value_view, preferred_element_type=jnp.float32)
    dscore = (near_prob * (dprob - inner_dot.reshape(-1, SEG)[:, :, None])).astype(jnp.bfloat16)
    grad_q = (
        jnp.einsum("gij,gjd->gid", dscore, key_view, preferred_element_type=jnp.float32) * inv_root
    )
    grad_k = (
        jnp.einsum("gij,gid->gjd", dscore, query_view, preferred_element_type=jnp.float32)
        * inv_root
    )
    grad_v = jnp.einsum(
        "gij,gid->gjd",
        near_prob.astype(jnp.bfloat16),
        grad_view,
        preferred_element_type=jnp.float32,
    )
    return (
        grad_q.reshape(row_count, -1),
        grad_k.reshape(row_count, -1),
        grad_v.reshape(row_count, -1),
    )


def far_grads(sel_query, far_keys, far_values, joint_sel, sel_grad, sel_inner):
    inv_root = sel_query.shape[1] ** (-0.5)
    far_scores = contract_cols(sel_query, far_keys) * inv_root
    far_prob = jnp.exp(far_scores - joint_sel[:, None])
    dprob = contract_cols(sel_grad, far_values)
    dscore = (far_prob * (dprob - sel_inner[:, None])).astype(jnp.bfloat16)
    grad_q = jnp.dot(dscore, far_keys, preferred_element_type=jnp.float32) * inv_root
    grad_k = contract_rows(dscore, sel_query) * inv_root
    grad_v = contract_rows(far_prob.astype(jnp.bfloat16), sel_grad)
    return (grad_q, grad_k, grad_v)


def inner_of(head_grad, head_attended):
    return jnp.sum(head_grad.astype(jnp.float32) * head_attended.astype(jnp.float32), axis=-1)


def backward_head(
    head_query,
    head_key,
    head_value,
    far_keys,
    far_values,
    offset,
    joint_lse,
    head_attended,
    head_grad,
):
    inner_dot = inner_of(head_grad, head_attended)
    near_q, near_k, near_v = near_grads(
        head_query, head_key, head_value, joint_lse, head_grad, inner_dot
    )
    far_q, far_k, far_v = far_grads(
        pick_rows(head_query, offset),
        far_keys,
        far_values,
        pick_rows(joint_lse, offset),
        pick_rows(head_grad, offset),
        pick_rows(inner_dot, offset),
    )
    return (near_q + place_rows(far_q, offset), near_k, near_v, far_k, far_v)


def forward_pack(parts):
    return forward_head(parts[0], parts[1], parts[2], parts[3], parts[4], parts[5])


def backward_pack(parts):
    return backward_head(
        parts[0], parts[1], parts[2], parts[3], parts[4], parts[5], parts[6], parts[7], parts[8]
    )


def body(queries, keys, values, offsets, w_out, grad_out):
    own_queries = queries[0]
    own_keys = keys[0]
    own_values = values[0]
    upstream = grad_out[0]
    row_count = own_queries.shape[0]
    head_q = split_heads(own_queries, HEADS)
    head_k = split_heads(own_keys, HEADS)
    head_v = split_heads(own_values, HEADS)
    far_k, far_v = (
        lax.all_gather(pick_all(own_keys, offsets), "ctx", axis=0, tiled=True),
        lax.all_gather(pick_all(own_values, offsets), "ctx", axis=0, tiled=True),
    )
    gathered_k = split_heads(far_k, HEADS)
    gathered_v = split_heads(far_v, HEADS)
    head_att, joint_lse = lax.map(
        forward_pack, (head_q, head_k, head_v, gathered_k, gathered_v, offsets)
    )
    attended = join_heads(head_att)
    output = jnp.dot(attended, w_out, preferred_element_type=jnp.float32).astype(jnp.bfloat16)
    dattend = contract_cols(upstream, w_out).astype(jnp.bfloat16)
    weight_total = lax.psum(contract_rows(attended, upstream), ("dp", "ctx"))
    grad_heads = split_heads(dattend, HEADS)
    model_width = own_queries.shape[1]
    grad_q, near_k, near_v, far_dk, far_dv = lax.map(
        backward_pack,
        (head_q, head_k, head_v, gathered_k, gathered_v, offsets, joint_lse, head_att, grad_heads),
    )
    far_terms = jnp.concatenate([join_heads(far_dk), join_heads(far_dv)], axis=1)
    own_terms = lax.psum_scatter(
        far_terms.astype(jnp.bfloat16), "ctx", scatter_dimension=0, tiled=True
    ).astype(jnp.float32)
    dquery = join_heads(grad_q)
    dkey = join_heads(near_k) + place_all(own_terms[:, :model_width], offsets)
    dvalue = join_heads(near_v) + place_all(own_terms[:, model_width:], offsets)
    total_rows = row_count * lax.axis_size("ctx") * lax.axis_size("dp")
    weight_grad = weight_total * total_rows ** (-0.5)
    return (
        output[None],
        dquery.astype(jnp.bfloat16)[None],
        dkey.astype(jnp.bfloat16)[None],
        dvalue.astype(jnp.bfloat16)[None],
        weight_grad,
    )


def solution(mesh):
    in_specs = (
        P("dp", "ctx", None),
        P("dp", "ctx", None),
        P("dp", "ctx", None),
        P(),
        P(),
        P("dp", "ctx", None),
    )
    out_specs = (
        P("dp", "ctx", None),
        P("dp", "ctx", None),
        P("dp", "ctx", None),
        P("dp", "ctx", None),
        P(),
    )
    return jax.shard_map(body, mesh=mesh, in_specs=in_specs, out_specs=out_specs, check_vma=False)
```

profile of v0, /device:TPU:1, one launch (start us, length us, event | category | flops | bytes accessed | tf_op | source)
XLA Modules:
  0.0 897.6 jit_solution(15339823454780444755)
XLA Ops:
  8.1 7.2 reshape_squeeze.17
  15.3 6.0 reshape_squeeze.19
  21.3 6.4 select_reduce_fusion
  36.8 4.8 copy.101
  44.8 4.7 copy.98
  55.3 24.4 %all-gather.3.cloned.1.call-done = bf16[1024,768]{1,0:T(8,128)(2,1)} async-done(((bf16[64,768]{1,0:T(8,128)(2,1)}), bf16[1024,768]{1,0:T(8,128)(2,1)}) %all-gather.3.cloned.1.call-update) | async-done | bytes 1572880 | tf_op jit(solution)/shard_map/all_gather | solution.py:207
  84.6 42.7 %all-gather.5.cloned.1.call-done = bf16[1024,768]{1,0:T(8,128)(2,1)} async-done(((bf16[64,768]{1,0:T(8,128)(2,1)}), bf16[1024,768]{1,0:T(8,128)(2,1)}) %all-gather.5.cloned.1.call-update) | async-done | bytes 1572880 | tf_op jit(solution)/shard_map/all_gather | solution.py:208
  132.2 263.3 %while.30 = (s32[]{:T(128)}, bf16[16,1024,48]{1,2,0:T(8,128)(2,1)}, f32[16,1024]{1,0:T(8,128)S(1)}, bf16[16,1024,48]{2,1,0:T(8,128)(2,1)}, bf16[16,1024,48]{2,1,...) while((s32[]{:T(128)}, bf16[16,1024,48]{1,2,0:T(8,128)(2,1)}, ...), condition=%wide.region_7.8_spmd, body=%wide.region_2.7_spmd.sunk | while | flops 222850000 | bytes 32720128 | solution.py:212
  144.9 3.7 fusion.138
  161.4 3.7 fusion.138
  177.8 3.7 fusion.138
  194.3 3.7 fusion.138
  210.7 3.7 fusion.138
  227.2 3.7 fusion.138
  243.6 3.7 fusion.138
  260.1 3.7 fusion.138
  276.5 3.7 fusion.138
  293.0 3.7 fusion.138
  309.5 3.7 fusion.138
  325.9 3.7 fusion.138
  342.4 3.7 fusion.138
  358.8 3.7 fusion.138
  375.3 3.7 fusion.138
  391.7 3.7 fusion.138
  395.4 4.3 fusion.81
  400.1 370.1 %while.31 = (s32[]{:T(128)}, bf16[16,1024,48]{1,2,0:T(8,128)(2,1)}, f32[16,1024,48]{1,2,0:T(8,128)}, f32[16,1024,48]{1,2,0:T(8,128)}, bf16[16,1024,48]{1,2,0:T(8...) while((s32[]{:T(128)}, bf16[16,1024,48]{1,2,0:T(8,128)(2,1)}, ...), condition=%wide.region_10.11_spmd, body=%wide.region_8.10_spmd.sunk | while | flops 544000000 | bytes 25185096 | solution.py:221
  777.5 3.8 fusion.84
  784.6 62.8 %reduce-scatter.2.cloned.1.call-done = bf16[64,1536]{1,0:T(8,128)(2,1)} async-done(((bf16[1024,1536]{1,0:T(8,128)(2,1)}), bf16[64,1536]{1,0:T(8,128)(2,1)}) %reduce-scatter.2.cloned.1.call-update) | async-done | bytes 196624 | tf_op jit(solution)/shard_map/reduce_scatter | solution.py:226
  848.9 8.4 broadcast_select_fusion
  857.3 7.7 select_n.135
  868.6 7.7 select_n.133
  879.9 6.9 fusion.79
  (1037 shorter events, 560.9 us)
Async XLA Ops:
  7.2 42.3 %copy-start = (bf16[1,1024,768]{2,1,0:T(8,128)(2,1)S(1)}, bf16[1,1024,768]{2,1,0:T(8,128)(2,1)}, u32[]{:S(2)}) copy-start(bf16[1,1024,768]{2,1,0:T(8,128)(2,1)} %param.15) | copy-start | bytes 4718596
  7.2 8.1 copy-start.4
  7.2 72.5 %all-gather.3.cloned.1.call-start = ((), (), s32[]{:S(2)}) async-start(), calls=%async_computation.1 | async-start | bytes 1671168 | tf_op jit(solution)/shard_map/all_gather | solution.py:207
  21.3 9.5 %copy-start.3 = (bf16[1,1024,768]{2,1,0:T(8,128)(2,1)S(1)}, bf16[1,1024,768]{2,1,0:T(8,128)(2,1)}, u32[]{:S(2)}) copy-start(bf16[1,1024,768]{2,1,0:T(8,128)(2,1)} %param.11) | copy-start | bytes 4718596
  29.5 97.7 %all-gather.5.cloned.1.call-start = ((), (), s32[]{:S(2)}) async-start(), calls=%async_computation.2 | async-start | bytes 1671168 | tf_op jit(solution)/shard_map/all_gather | solution.py:208
  30.5 750.8 %all-reduce.2.cloned.1.call-start = ((), (), s32[]{:S(2)}) async-start(), calls=%async_computation.4 | async-start | bytes 4718592 | tf_op jit(solution)/shard_map/psum | solution.py:218
  32.4 2.7 copy-start.6
  36.8 4.8 copy-start.5
  129.0 3.2 copy-start.10
  139.9 2.0 copy-start.2
  156.4 2.0 copy-start.2
  172.8 2.0 copy-start.2
  189.3 2.0 copy-start.2
  205.8 2.0 copy-start.2
  222.2 2.0 copy-start.2
  238.7 2.0 copy-start.2
  255.1 2.0 copy-start.2
  271.6 2.0 copy-start.2
  288.0 2.0 copy-start.2
  304.5 2.0 copy-start.2
  320.9 2.0 copy-start.2
  337.4 2.0 copy-start.2
  353.9 2.0 copy-start.2
  370.3 2.0 copy-start.2
  386.8 2.0 copy-start.2
  395.4 4.6 copy-start.7
  399.8 447.6 %reduce-scatter.2.cloned.1.call-start = ((), (), s32[]{:S(2)}) async-start(), calls=%async_computation.3 | async-start | bytes 3342336 | tf_op jit(solution)/shard_map/reduce_scatter | solution.py:226
  774.5 1.4 copy-start.8
  774.5 3.0 copy-start.9
  886.8 4.3 copy-start.1
Sparse Core Ops, SparseCore 0:
  29.7 49.9 all-gather.2
  82.1 45.0 all-gather.4
  399.9 149.7 all-reduce.1
  774.7 72.6 reduce-scatter.1
where the time goes:
time: 907 us; the launch traced here: 898 us
  matrix products  370 us (41%)
  local copies, waits for them, and re-layouts  234 us (26%)
  waiting for transfers between devices  130 us (14%)
  other arithmetic  83.7 us (9%)
  loops' own time  65.7 us (7%)
  between operations  13.9 us (2%)
    dynamic_slice x96, local copies, waits for them, and re-layouts, body(): lax.map(forward_pack, (head_q, head_k, head_v, gathered_k, gathered_v, of...  66.9 us
    reduce_scatter x1, waiting for transfers between devices, body(): lax.psum_scatter(far_terms.astype(jnp.bfloat16), 'ctx', scatter_dimension...  62.8 us
    dot_general x49, matrix products, contract_cols(): lax.dot_general(left, right, (((1,), (1,)), ((), ())), preferred_element_...  61.5 us
    dot_general x16, matrix products, near_output(): jnp.einsum('gij,gjd->gid', near_prob, segment_view(head_value), preferred...  59.3 us
    all_gather x1, waiting for transfers between devices, body(): lax.all_gather(pick_all(own_values, offsets), 'ctx', axis=0, tiled=True)  42.7 us
    dot_general x16, matrix products, near_grads(): jnp.einsum('gij,gjd->gid', dscore, key_view, preferred_element_type=jnp.f...  37.5 us
    dot_general x16, matrix products, near_grads(): jnp.einsum('gij,gid->gjd', dscore, query_view, preferred_element_type=jnp...  34.5 us
    while x64, local copies, waits for them, and re-layouts  33.6 us
  transfers between devices with their start and end apart: 4, of which 3 were waited for; matrix products, arithmetic and copies ran while one was open for 42% of the time, Pallas kernels for 0%

commit v1 on v0

v1 whole, which is shorter than its diff:
```python
import functools

import jax
import jax.numpy as jnp
from jax import lax
from jax.experimental import pallas as pl
from jax.experimental.pallas import tpu as pltpu
from jax.sharding import PartitionSpec as P

HEADS = 16
HEAD = 48
ROWS = 1024
RATE = 16
PICKED = ROWS // RATE
WIDTH = 768
GROUP = 8
COLS = GROUP * HEAD
PACK = 256
CHUNK = 256
ROOT = HEAD**-0.5
SCALE = ROOT * 1.4426950408889634
BF = jnp.bfloat16
F32 = jnp.float32
VMEM_LIMIT = 56 << 20


def dot(left, right):
    return lax.dot_general(left, right, (((1,), (0,)), ((), ())), preferred_element_type=F32)


def dot_t(left, right):
    return lax.dot_general(left, right, (((1,), (1,)), ((), ())), preferred_element_type=F32)


def split2(x):
    hi = x.astype(BF)
    return hi, (x - hi.astype(F32)).astype(BF)


def split3(x):
    hi = x.astype(BF)
    rest = x - hi.astype(F32)
    mid = rest.astype(BF)
    return hi.astype(F32), mid.astype(F32), rest - mid.astype(F32)


def rows16(parts):
    which = lax.broadcasted_iota(jnp.int32, (16, parts[0].shape[1]), 0)
    out = jnp.zeros(which.shape, F32)
    for row, part in enumerate(parts):
        out = jnp.where(which == row, part, out)
    return out


def selector(offset):
    row = lax.broadcasted_iota(jnp.int32, (PICKED, ROWS), 0)
    col = lax.broadcasted_iota(jnp.int32, (PICKED, ROWS), 1)
    return jnp.where(col == row * RATE + offset, 1.0, 0.0).astype(BF)


def attend(query, key, value, e_ref):
    hi, lo = split2(query.astype(F32) * SCALE)
    pad = jnp.zeros((32, ROWS), BF)
    right = jnp.concatenate([hi, lo, pad], axis=0)
    left = jnp.concatenate([key, key, pad], axis=0).T
    weights = jnp.concatenate([value, jnp.ones((16, ROWS), BF)], axis=0)
    tops, sums = [], []
    for start in range(0, ROWS, CHUNK):
        score = dot(left, right[:, start : start + CHUNK])
        top = jnp.max(score, axis=0, keepdims=True)
        e = jnp.exp2(score - top).astype(BF)
        e_ref[:, start : start + CHUNK] = e
        tops.append(top)
        sums.append(dot(weights, e))
    return jnp.concatenate(tops, axis=1), jnp.concatenate(sums, axis=1)


def gradients(e_ref, query, key, value, dattend, ratio, inner, ds_ref):
    hi, lo = split2(dattend * ratio)
    ihi, ilo = split2(-inner * ratio)
    tail = rows16([ihi.astype(F32), ilo.astype(F32)]).astype(BF)
    pad = jnp.zeros((16, ROWS), BF)
    right = jnp.concatenate([hi, lo, tail, pad], axis=0)
    one = jnp.ones((1, ROWS), F32)
    left = jnp.concatenate([value, value, rows16([one, one]).astype(BF), pad], axis=0).T
    dqs = []
    for start in range(0, ROWS, CHUNK):
        cols = slice(start, start + CHUNK)
        d = dot(left, right[:, cols]).astype(BF) * e_ref[:, cols]
        ds_ref[:, cols] = d
        dqs.append(dot(key, d))
    dq = jnp.concatenate(dqs, axis=1) * ROOT
    dk = dot_t(query, ds_ref[...]) * ROOT
    dv = dot_t(hi, e_ref[...])
    return dq, dk, dv


def prologue_kernel(off_ref, q_ref, k_ref, v_ref, g_ref, w_ref, qt_ref, kt_ref, vt_ref, dt_ref, pack_ref):
    group = pl.program_id(0)
    qt_ref[...] = q_ref[...].T
    kt_ref[...] = k_ref[...].T
    vt_ref[...] = v_ref[...].T
    dt_ref[...] = dot_t(w_ref[...], g_ref[...]).astype(BF)
    lane = lax.broadcasted_iota(jnp.int32, (PICKED, PACK), 1)
    spot_row = lax.broadcasted_iota(jnp.int32, (HEAD, PACK), 0)
    spot_col = lax.broadcasted_iota(jnp.int32, (HEAD, PACK), 1)
    spot = jnp.where(spot_col == spot_row + 4 * HEAD, 1.0, 0.0).astype(BF)
    for h in range(GROUP):
        rows = slice(h * HEAD, (h + 1) * HEAD)
        pick = selector(off_ref[group * GROUP + h])
        key, value = kt_ref[rows, :], vt_ref[rows, :]
        stack = jnp.concatenate(
            [qt_ref[rows, :], key, value, dt_ref[rows, :], jnp.zeros((PACK - 4 * HEAD, ROWS), BF)], axis=0
        )
        picked = dot_t(pick, stack)
        hi, lo = split2(picked[:, :HEAD] * SCALE)
        score = dot(hi, key) + dot(lo, key)
        top = jnp.max(score, axis=1, keepdims=True)
        e = jnp.exp2(score - top)
        total = jnp.sum(e, axis=1, keepdims=True)
        near = dot_t(e.astype(BF), value) / total
        out = picked + dot(near.astype(BF), spot)
        for place, part in enumerate(split3(top) + split3(total)):
            out = jnp.where(lane == 5 * HEAD + place, part, out)
        pack_ref[h] = out.astype(BF)


def forward_kernel(q_ref, k_ref, v_ref, e_ref, att_ref, stat_ref):
    top, sums = attend(q_ref[...], k_ref[...], v_ref[...], e_ref.at[0])
    recip = 1.0 / sums[HEAD : HEAD + 1, :]
    att_ref[...] = (sums[:HEAD, :] * recip).astype(BF)
    stat_ref[0, 0:1, :] = top
    stat_ref[0, 1:2, :] = recip


def far_kernel(in_ref, out_ref, e_ref, ds_ref):
    packed = in_ref[...].T
    query, key, value = (packed[i * HEAD : (i + 1) * HEAD] for i in range(3))
    dattend = packed[3 * HEAD : 4 * HEAD].astype(F32)
    near_att = packed[4 * HEAD : 5 * HEAD].astype(F32)
    tail = packed[5 * HEAD :].astype(F32)
    near_top = tail[0:1] + tail[1:2] + tail[2:3]
    near_total = tail[3:4] + tail[4:5] + tail[5:6]
    far_top, sums = attend(query, key, value, e_ref)
    top = jnp.maximum(near_top, far_top)
    near_part = near_total * jnp.exp2(near_top - top)
    far_scale = jnp.exp2(far_top - top)
    total = near_part + sums[HEAD : HEAD + 1, :] * far_scale
    recip = 1.0 / total
    att = ((near_att * near_part + sums[:HEAD, :] * far_scale) * recip).astype(BF)
    inner = jnp.sum(att.astype(F32) * dattend, axis=0, keepdims=True)
    dq, dk, dv = gradients(e_ref, query, key, value, dattend, far_scale * recip, inner, ds_ref)
    scalars = rows16(split3(top + jnp.log2(total)) + split3(inner)).astype(BF)
    back = jnp.concatenate(
        [dq.astype(BF), dk.astype(BF), dv.astype(BF), att, scalars, jnp.zeros((PACK - 4 * HEAD - 16, ROWS), BF)], axis=0
    )
    out_ref[...] = back.T


def output_kernel(off_ref, att_ref, back_ref, w_ref, g_ref, full_ref, out_ref, wg_ref, acc_ref):
    group = pl.program_id(0)
    tile = lax.broadcasted_iota(jnp.int32, (HEAD, ROWS), 1) % RATE
    for h in range(GROUP):
        rows = slice(h * HEAD, (h + 1) * HEAD)
        offset = off_ref[group * GROUP + h]
        back = back_ref[h].T[3 * HEAD : 4 * HEAD]
        placed = dot(back, selector(offset)).astype(BF)
        full_ref[rows, :] = jnp.where(tile == offset, placed, att_ref[rows, :])
    att = full_ref[...]
    wg_ref[...] = dot(att, g_ref[...]).astype(BF)
    part = dot(att.T, w_ref[...])

    @pl.when(group == 0)
    def _():
        acc_ref[...] = part

    @pl.when(group == pl.num_programs(0) - 1)
    def _():
        out_ref[...] = (acc_ref[...] + part).astype(BF)


def backward_kernel(
    off_ref, e_ref, q_ref, k_ref, v_ref, d_ref, att_ref, stat_ref, back_ref, dq_ref, dk_ref, dv_ref, ds_ref, tq_ref, tk_ref, tv_ref
):
    h = pl.program_id(1)
    offset = off_ref[pl.program_id(0) * GROUP + h]
    placed = dot(back_ref[0].T, selector(offset))
    tail = placed[4 * HEAD : 4 * HEAD + 8]
    joint = tail[0:1] + tail[1:2] + tail[2:3]
    far_inner = tail[3:4] + tail[4:5] + tail[5:6]
    dilated = lax.broadcasted_iota(jnp.int32, (1, ROWS), 1) % RATE == offset
    dattend = d_ref[...].astype(F32)
    ratio = jnp.where(dilated, jnp.exp2(jnp.where(dilated, stat_ref[0, 0:1, :] - joint, 0.0)), stat_ref[0, 1:2, :])
    inner = jnp.sum(dattend * att_ref[...].astype(F32), axis=0, keepdims=True)
    inner = jnp.where(dilated, far_inner, inner)
    dq, dk, dv = gradients(e_ref.at[0], q_ref[...], k_ref[...], v_ref[...], dattend, ratio, inner, ds_ref)
    rows = pl.ds(pl.multiple_of(h * HEAD, 16), HEAD)
    tq_ref[rows, :] = (dq + placed[:HEAD]).astype(BF)
    tk_ref[rows, :] = (dk + placed[HEAD : 2 * HEAD]).astype(BF)
    tv_ref[rows, :] = (dv + placed[2 * HEAD : 3 * HEAD]).astype(BF)

    @pl.when(h == GROUP - 1)
    def _():
        dq_ref[...] = tq_ref[...].T
        dk_ref[...] = tk_ref[...].T
        dv_ref[...] = tv_ref[...].T


def params():
    return pltpu.CompilerParams(vmem_limit_bytes=VMEM_LIMIT)


def cost(flops, moved, exps=0):
    return pl.CostEstimate(flops=flops, bytes_accessed=moved, transcendentals=exps)


HEAD_FLOPS = 2 * ROWS * ROWS * 256


def prologue(offsets, q, k, v, g, w):
    nat = pl.BlockSpec((ROWS, COLS), lambda i, o: (0, i))
    tr = pl.BlockSpec((COLS, ROWS), lambda i, o: (i, 0))
    shape = jax.ShapeDtypeStruct((WIDTH, ROWS), BF)
    return pl.pallas_call(
        prologue_kernel,
        grid_spec=pltpu.PrefetchScalarGridSpec(
            num_scalar_prefetch=1,
            grid=(HEADS // GROUP,),
            in_specs=[nat, nat, nat, pl.BlockSpec((ROWS, WIDTH), lambda i, o: (0, 0)), pl.BlockSpec((COLS, WIDTH), lambda i, o: (i, 0))],
            out_specs=[tr, tr, tr, tr, pl.BlockSpec((GROUP, PICKED, PACK), lambda i, o: (i, 0, 0))],
        ),
        out_shape=[shape] * 4 + [jax.ShapeDtypeStruct((HEADS, PICKED, PACK), BF)],
        compiler_params=params(),
        cost_estimate=cost(4 * HEAD_FLOPS, 14 << 20, 1 << 20),
        name="prologue",
    )(offsets, q, k, v, g, w)


def forward(qt, kt, vt, first, count):
    spec = pl.BlockSpec((HEAD, ROWS), lambda i: (i + first, 0))
    return pl.pallas_call(
        forward_kernel,
        grid=(count,),
        in_specs=[spec] * 3,
        out_specs=[
            pl.BlockSpec((1, ROWS, ROWS), lambda i: (i, 0, 0)),
            pl.BlockSpec((HEAD, ROWS), lambda i: (i, 0)),
            pl.BlockSpec((1, 8, ROWS), lambda i: (i, 0, 0)),
        ],
        out_shape=[
            jax.ShapeDtypeStruct((count, ROWS, ROWS), BF),
            jax.ShapeDtypeStruct((count * HEAD, ROWS), BF),
            jax.ShapeDtypeStruct((count, 8, ROWS), F32),
        ],
        compiler_params=params(),
        cost_estimate=cost(2 * count * HEAD_FLOPS, count * (2 << 20), count << 20),
        name="near_forward",
    )(qt, kt, vt)


def far(packed):
    return pl.pallas_call(
        far_kernel,
        out_shape=jax.ShapeDtypeStruct((ROWS, PACK), BF),
        scratch_shapes=[pltpu.VMEM((ROWS, ROWS), BF), pltpu.VMEM((ROWS, ROWS), BF)],
        compiler_params=params(),
        cost_estimate=cost(6 * HEAD_FLOPS, 1 << 20, 1 << 20),
        name="far",
    )(packed)


def project(offsets, att, back, w, g):
    return pl.pallas_call(
        output_kernel,
        grid_spec=pltpu.PrefetchScalarGridSpec(
            num_scalar_prefetch=1,
            grid=(HEADS // GROUP,),
            in_specs=[
                pl.BlockSpec((COLS, ROWS), lambda i, o: (i, 0)),
                pl.BlockSpec((GROUP, PICKED, PACK), lambda i, o: (i, 0, 0)),
                pl.BlockSpec((COLS, WIDTH), lambda i, o: (i, 0)),
                pl.BlockSpec((ROWS, WIDTH), lambda i, o: (0, 0)),
            ],
            out_specs=[
                pl.BlockSpec((COLS, ROWS), lambda i, o: (i, 0)),
                pl.BlockSpec((ROWS, WIDTH), lambda i, o: (0, 0)),
                pl.BlockSpec((COLS, WIDTH), lambda i, o: (i, 0)),
            ],
            scratch_shapes=[pltpu.VMEM((ROWS, WIDTH), F32)],
        ),
        out_shape=[
            jax.ShapeDtypeStruct((WIDTH, ROWS), BF),
            jax.ShapeDtypeStruct((ROWS, WIDTH), BF),
            jax.ShapeDtypeStruct((WIDTH, WIDTH), BF),
        ],
        compiler_params=params(),
        cost_estimate=cost(4 * ROWS * WIDTH * WIDTH, 10 << 20),
        name="project",
    )(offsets, att, back, w, g)


def backward(offsets, e, qt, kt, vt, dt, att, stat, back, first, count):
    spec = pl.BlockSpec((HEAD, ROWS), lambda g, h, o: (first + g * GROUP + h, 0))
    out = pl.BlockSpec((ROWS, COLS), lambda g, h, o: (0, g))
    here = lambda g, h, o: (g * GROUP + h, 0, 0)
    return pl.pallas_call(
        backward_kernel,
        grid_spec=pltpu.PrefetchScalarGridSpec(
            num_scalar_prefetch=1,
            grid=(count // GROUP, GROUP),
            in_specs=[pl.BlockSpec((1, ROWS, ROWS), here)]
            + [spec] * 4
            + [
                pl.BlockSpec((HEAD, ROWS), lambda g, h, o: (g * GROUP + h, 0)),
                pl.BlockSpec((1, 8, ROWS), here),
                pl.BlockSpec((1, PICKED, PACK), lambda g, h, o: (first + g * GROUP + h, 0, 0)),
            ],
            out_specs=[out] * 3,
            scratch_shapes=[pltpu.VMEM((ROWS, ROWS), BF)] + [pltpu.VMEM((COLS, ROWS), BF)] * 3,
        ),
        out_shape=[jax.ShapeDtypeStruct((ROWS, count * HEAD), BF)] * 3,
        compiler_params=params(),
        cost_estimate=cost(4 * count * HEAD_FLOPS, count * (2 << 20)),
        name="near_backward",
    )(offsets[first : first + count], e, qt, kt, vt, dt, att, stat, back)


def body(queries, keys, values, offsets, w_out, grad_out):
    upstream = grad_out[0]
    qt, kt, vt, dt, packed = prologue(offsets, queries[0], keys[0], values[0], upstream, w_out)
    arrived = lax.all_to_all(packed, "ctx", 0, 0, tiled=True)
    half = HEADS // 2
    e0, att0, stat0 = forward(qt, kt, vt, 0, half)
    far_out = far(arrived.reshape(ROWS, PACK)).reshape(HEADS, PICKED, PACK)
    back = lax.all_to_all(far_out, "ctx", 0, 0, tiled=True)
    e1, att1, stat1 = forward(qt, kt, vt, half, half)
    _, output, weight_part = project(offsets, jnp.concatenate([att0, att1], axis=0), back, w_out, upstream)
    devices = lax.axis_size("dp") * lax.axis_size("ctx")
    pieces = lax.all_to_all(weight_part.reshape(devices, WIDTH // devices, WIDTH), ("dp", "ctx"), 0, 0, tiled=True)
    first = backward(offsets, e0, qt, kt, vt, dt, att0, stat0, back, 0, half)
    total = jnp.sum(pieces.astype(F32), axis=0).astype(BF)
    whole = lax.all_to_all(jnp.broadcast_to(total[None], pieces.shape), ("dp", "ctx"), 0, 0, tiled=True)
    second = backward(offsets, e1, qt, kt, vt, dt, att1, stat1, back, half, half)
    weight_grad = whole.reshape(WIDTH, WIDTH).astype(F32) * (ROWS * devices) ** -0.5
    dq, dk, dv = (jnp.concatenate(pair, axis=1) for pair in zip(first, second))
    return output[None], dq[None], dk[None], dv[None], weight_grad


def solution(mesh):
    rows = P("dp", "ctx", None)
    return jax.shard_map(
        body,
        mesh=mesh,
        in_specs=(rows, rows, rows, P(), P(), rows),
        out_specs=(rows, rows, rows, rows, P()),
        check_vma=False,
    )
```

time: 907 us -> 202 us (0.22)
  matrix products: 370 us -> 0 us
  local copies, waits for them, and re-layouts: 234 us -> 8.29 us
  Pallas kernels: 0 us -> 147 us
  waiting for transfers between devices: 130 us -> 0.01 us
  other arithmetic: 83.7 us -> 9 us
  loops' own time: 65.7 us -> 0 us
  starting transfers between devices: 0.56 us -> 36.1 us
  between operations: 13.9 us -> 0.73 us
    dot_general x227 -> x0, matrix products: 370 us -> none  [the longest x49 61.5 us: contract_cols(): lax.dot_general(left, right, (((1,), (1,)), ((), ())), preferred_element_...]
    pallas_call x0 -> x7, Pallas kernels: none -> 147 us  [the longest x2 60.5 us: backward(): pl.pallas_call(backward_kernel, grid_spec=pltpu.PrefetchScalarGridSpec(nu...]
    dynamic_slice x240 -> x0, local copies, waits for them, and re-layouts: 96.4 us -> none  [the longest x96 66.9 us: body(): lax.map(forward_pack, (head_q, head_k, head_v, gathered_k, gathered_v, of...]
    all_gather x2 -> x0, waiting for transfers between devices: 67.1 us -> none  [the longest x1 42.7 us: body(): lax.all_gather(pick_all(own_values, offsets), 'ctx', axis=0, tiled=True)]
    another operation x2 -> x0, loops' own time: 65.7 us -> none  [the longest x1 32.9 us: body(): lax.map(forward_pack, (head_q, head_k, head_v, gathered_k, gathered_v, of...]
    reduce_scatter x1 -> x0, waiting for transfers between devices: 62.8 us -> none  [body(): lax.psum_scatter(far_terms.astype(jnp.bfloat16), 'ctx', scatter_dimension...]
    while x69 -> x0, local copies, waits for them, and re-layouts: 52.6 us -> none
    reduce_sum x49 -> x1, other arithmetic: 40.3 us -> 0.36 us  [body(): total = jnp.sum(pieces.astype(F32), axis=0).astype(BF)]
  transfers between devices with their start and end apart: 4 -> 4, of which waited for: 3 -> 0; matrix products, arithmetic and copies ran while one was open for 42% -> 4% of each run, Pallas kernels for 0% -> 56%
where the time goes in v1:
time: 202 us; the launch traced here: 201 us
  Pallas kernels  147 us (73%)
  starting transfers between devices  36.1 us (18%)
  other arithmetic  9 us (4%)
  local copies, waits for them, and re-layouts  8.29 us (4%)
    pallas_call x2, Pallas kernels, backward(): pl.pallas_call(backward_kernel, grid_spec=pltpu.PrefetchScalarGridSpec(nu...  60.5 us
    pallas_call x2, Pallas kernels, forward(): pl.pallas_call(forward_kernel, grid=(count,), in_specs=[spec] * 3, out_sp...  52.1 us
    pallas_call x1, Pallas kernels, prologue(): pl.pallas_call(prologue_kernel, grid_spec=pltpu.PrefetchScalarGridSpec(nu...  17.9 us
    all_to_all x1, starting transfers between devices, body(): lax.all_to_all(jnp.broadcast_to(total[None], pieces.shape), ('dp', 'ctx')...  10.2 us
    all_to_all x1, starting transfers between devices, body(): lax.all_to_all(weight_part.reshape(devices, WIDTH // devices, WIDTH), ('d...  9.43 us
    all_to_all x1, starting transfers between devices, body(): arrived = lax.all_to_all(packed, 'ctx', 0, 0, tiled=True)  9.29 us
    pallas_call x1, Pallas kernels, project(): pl.pallas_call(output_kernel, grid_spec=pltpu.PrefetchScalarGridSpec(num_...  8.78 us
    pallas_call x1, Pallas kernels, far(): pl.pallas_call(far_kernel, out_shape=jax.ShapeDtypeStruct((ROWS, PACK), B...  7.94 us
  transfers between devices with their start and end apart: 4, of which 0 were waited for; matrix products, arithmetic and copies ran while one was open for 4% of the time, Pallas kernels for 56%

profile of v1, /device:TPU:1, one launch (start us, length us, event | category | flops | bytes accessed | tf_op | source)
XLA Modules:
  0.0 201.4 jit_solution(3398968081240569664)
XLA Ops:
  0.6 17.9 %prologue.1 = (bf16[768,1024]{1,0:T(8,128)(2,1)}, bf16[768,1024]{1,0:T(8,128)(2,1)}, bf16[768,1024]{1,0:T(8,128)(2,1)}, bf16[768,1024]{1,0:T(8,128)(2,1)}, bf16[16,64,256]{2,1,0:T(8,128)(2,1)}) custom-call(s32[16]{0:T(128)} %off_ref.3, bf16[1024,768]{1,0:T(8,128)(2,1)} %bitcast.15, bf16[1024,768]{1,0:T(8,128)(2,1)} %bitcast.16, bf16[1024,768]{1,0:T(8,128)(2,1)} %bitcast.17, ...), custom_call_target="tpu_custom_call" | custom-call | flops 2147483648 | bytes 14680064 | tf_op jit(solution)/shard_map/prologue/pallas_call | solution.py:224
  18.5 9.3 %all-to-all-start = ((bf16[16,64,256]{2,1,0:T(8,128)(2,1)}), bf16[16,64,256]{2,1,0:T(8,128)(2,1)S(1)}, u32[]{:S(2)}, u32[]{:S(2)}) async-start(bf16[16,64,256]{2,1,0:T(8,128)(2,1)} %get-tuple-element.29), calls=%async_computation | async-start | bytes 1048576 | tf_op jit(solution)/shard_map/all_to_all | solution.py:331
  27.8 26.0 %near_forward.3 = (bf16[8,1024,1024]{2,1,0:T(8,128)(2,1)}, bf16[384,1024]{1,0:T(8,128)(2,1)}, f32[8,8,1024]{2,1,0:T(8,128)}) custom-call(bf16[768,1024]{1,0:T(8,128)(2,1)} %get-tuple-element.24.q_ref, bf16[768,1024]{1,0:T(8,128)(2,1)} %get-tuple-element.25.k_ref, bf16[768,1024]{1,0:T(8,128)(2,1)} %get-tuple-element.26.v_ref), custom_call_target="tpu_custom_call" | custom-call | flops 8589934592 | bytes 16777216 | tf_op jit(solution)/shard_map/near_forward/pallas_call | solution.py:241
  53.8 0.0 all-to-all-done
  53.8 0.8 copy-done.7
  54.6 7.9 %far.1 = bf16[1024,256]{1,0:T(8,128)(2,1)} custom-call(bf16[1024,256]{1,0:T(8,128)(2,1)} %bitcast.13), custom_call_target="tpu_custom_call" | custom-call | flops 3221225472 | bytes 1048576 | tf_op jit(solution)/shard_map/far/pallas_call | solution.py:262
  62.6 7.2 %all-to-all-start.1 = ((bf16[16,64,256]{2,1,0:T(8,128)(2,1)}), bf16[16,64,256]{2,1,0:T(8,128)(2,1)S(1)}, u32[]{:S(2)}, u32[]{:S(2)}) async-start(bf16[16,64,256]{2,1,0:T(8,128)(2,1)} %bitcast.14), calls=%async_computation.1 | async-start | bytes 1048576 | tf_op jit(solution)/shard_map/all_to_all | solution.py:335
  69.8 26.1 %near_forward.2 = (bf16[8,1024,1024]{2,1,0:T(8,128)(2,1)}, bf16[384,1024]{1,0:T(8,128)(2,1)}, f32[8,8,1024]{2,1,0:T(8,128)}) custom-call(bf16[768,1024]{1,0:T(8,128)(2,1)} %get-tuple-element.24.q_ref, bf16[768,1024]{1,0:T(8,128)(2,1)} %get-tuple-element.25.k_ref, bf16[768,1024]{1,0:T(8,128)(2,1)} %get-tuple-element.26.v_ref), custom_call_target="tpu_custom_call" | custom-call | flops 8589934592 | bytes 16777216 | tf_op jit(solution)/shard_map/near_forward/pallas_call | solution.py:241
  95.9 0.0 copy-done.4
  95.9 2.4 %pad_maximum_fusion.att_ref = bf16[768,1024]{1,0:T(8,128)(2,1)} fusion(bf16[384,1024]{1,0:T(8,128)(2,1)S(1)} %copy-done.4, bf16[384,1024]{1,0:T(8,128)(2,1)} %get-tuple-element.27.att_ref), kind=kLoop, calls=%fused_computation.1 | loop fusion | flops 3145728 | bytes 3145728 | tf_op jit(solution)/shard_map/concatenate | solution.py:337
  98.3 0.0 copy-done.8
  98.3 0.6 fusion
  98.9 0.0 all-to-all-done.1.back_ref
  98.9 0.8 copy-done.6
  99.7 8.8 %project.1 = (bf16[768,1024]{1,0:T(8,128)(2,1)}, bf16[1024,768]{1,0:T(8,128)(2,1)}, bf16[768,768]{1,0:T(8,128)(2,1)}) custom-call(s32[16]{0:T(128)} %off_ref.3, bf16[768,1024]{1,0:T(8,128)(2,1)} %pad_maximum_fusion.att_ref, bf16[16,64,256]{2,1,0:T(8,128)(2,1)} %copy-done.6, bf16[768,768]{1,0:T(8,128)(2,1)} %w_ref.3, bf16[1024,768]{1,0:T(8,128)(2,1)} %bitcast.19), custom_call_target="tpu_custom_call" | custom-call | flops 2415919104 | bytes 10485760 | tf_op jit(solution)/shard_map/project/pallas_call | solution.py:273
  108.5 3.2 %reshape.26 = bf16[128,6,768]{2,1,0:T(8,128)(2,1)} reshape(bf16[768,768]{1,0:T(8,128)(2,1)} %get-tuple-element.42) | data formatting | bytes 2359296 | tf_op jit(solution)/shard_map/reshape | solution.py:339
  111.7 9.4 %all-to-all-start.2 = ((bf16[128,6,768]{2,1,0:T(8,128)(2,1)}), bf16[128,6,768]{2,1,0:T(8,128)(2,1)S(1)}, u32[]{:S(2)}, u32[]{:S(2)}) async-start(bf16[128,6,768]{2,1,0:T(8,128)(2,1)} %reshape.26), calls=%async_computation.2 | async-start | bytes 3145728 | tf_op jit(solution)/shard_map/all_to_all | solution.py:339
  121.2 30.2 %near_backward.3 = (bf16[1024,384]{1,0:T(8,128)(2,1)}, bf16[1024,384]{1,0:T(8,128)(2,1)}, bf16[1024,384]{1,0:T(8,128)(2,1)}) custom-call(s32[8]{0:T(128)} %get-tuple-element.44.off_ref, bf16[8,1024,1024]{2,1,0:T(8,128)(2,1)} %get-tuple-element.35.e_ref, bf16[768,1024]{1,0:T(8,128)(2,1)} %get-tuple-element.24.q_ref, ...), custom_call_target="tpu_custom_call" | custom-call | flops 17179869184 | bytes 16777216 | tf_op jit(solution)/shard_map/near_backward/pallas_call | solution.py:306
  151.4 0.0 all-to-all-done.2
  151.4 0.4 reduce_sum.12
  151.7 1.3 broadcast_in_dim.22
  153.0 10.2 %all-to-all-start.3 = ((bf16[128,6,768]{2,1,0:T(8,128)(2,1)}), bf16[128,6,768]{2,1,0:T(8,128)(2,1)}, u32[]{:S(2)}, u32[]{:S(2)}) async-start(bf16[128,6,768]{2,1,0:T(8,128)(2,1)} %broadcast_in_dim.22), calls=%async_computation.3 | async-start | bytes 3145728 | tf_op jit(solution)/shard_map/all_to_all | solution.py:342
  163.2 30.3 %near_backward.2 = (bf16[1024,384]{1,0:T(8,128)(2,1)}, bf16[1024,384]{1,0:T(8,128)(2,1)}, bf16[1024,384]{1,0:T(8,128)(2,1)}) custom-call(s32[8]{0:T(128)} %get-tuple-element.43.off_ref, bf16[8,1024,1024]{2,1,0:T(8,128)(2,1)} %get-tuple-element.31.e_ref, bf16[768,1024]{1,0:T(8,128)(2,1)} %get-tuple-element.24.q_ref, ...), custom_call_target="tpu_custom_call" | custom-call | flops 17179869184 | bytes 16777216 | tf_op jit(solution)/shard_map/near_backward/pallas_call | solution.py:306
  193.5 0.0 copy-start
  193.5 0.0 copy-start.1
  193.5 0.0 copy-start.2
  193.5 0.0 copy-start.3
  193.5 2.6 %maximum_bitcast_fusion.2 = bf16[1,1024,768]{2,1,0:T(8,128)(2,1)} fusion(bf16[1024,384]{1,0:T(8,128)(2,1)S(1)} %copy-done.5, bf16[1024,384]{1,0:T(8,128)(2,1)} %get-tuple-element.40), kind=kLoop, calls=%fused_computation.4 | loop fusion | flops 3145728 | bytes 3145728 | tf_op jit(solution)/shard_map/broadcast_in_dim | solution.py:346
  196.1 1.9 maximum_bitcast_fusion
  198.0 0.0 all-to-all-done.3
  198.0 1.8 convert_multiply_fusion
  199.8 1.6 mul.11
  (10 shorter events, 0.0 us)
Async XLA Ops:
  18.5 35.3 %all-to-all-start = ((bf16[16,64,256]{2,1,0:T(8,128)(2,1)}), bf16[16,64,256]{2,1,0:T(8,128)(2,1)S(1)}, u32[]{:S(2)}, u32[]{:S(2)}) async-start(bf16[16,64,256]{2,1,0:T(8,128)(2,1)} %get-tuple-element.29), calls=%async_computation | async-start | bytes 1048576 | tf_op jit(solution)/shard_map/all_to_all | solution.py:331
  53.8 0.8 copy-start.7
  62.6 36.3 %all-to-all-start.1 = ((bf16[16,64,256]{2,1,0:T(8,128)(2,1)}), bf16[16,64,256]{2,1,0:T(8,128)(2,1)S(1)}, u32[]{:S(2)}, u32[]{:S(2)}) async-start(bf16[16,64,256]{2,1,0:T(8,128)(2,1)} %bitcast.14), calls=%async_computation.1 | async-start | bytes 1048576 | tf_op jit(solution)/shard_map/all_to_all | solution.py:335
  69.8 26.1 %copy-start.4 = (bf16[384,1024]{1,0:T(8,128)(2,1)S(1)}, bf16[384,1024]{1,0:T(8,128)(2,1)}, u32[]{:S(2)}) copy-start(bf16[384,1024]{1,0:T(8,128)(2,1)} %get-tuple-element.28.att_ref) | copy-start | bytes 2359300
  95.9 2.4 %copy-start.8 = (s32[16]{0:T(128)S(1)}, s32[16]{0:T(128)}, u32[]{:S(2)}) copy-start(s32[16]{0:T(128)} %off_ref.3) | copy-start | bytes 196
  98.9 0.8 copy-start.6
  111.7 39.6 %all-to-all-start.2 = ((bf16[128,6,768]{2,1,0:T(8,128)(2,1)}), bf16[128,6,768]{2,1,0:T(8,128)(2,1)S(1)}, u32[]{:S(2)}, u32[]{:S(2)}) async-start(bf16[128,6,768]{2,1,0:T(8,128)(2,1)} %reshape.26), calls=%async_computation.2 | async-start | bytes 3145728 | tf_op jit(solution)/shard_map/all_to_all | solution.py:339
  153.0 45.0 %all-to-all-start.3 = ((bf16[128,6,768]{2,1,0:T(8,128)(2,1)}), bf16[128,6,768]{2,1,0:T(8,128)(2,1)}, u32[]{:S(2)}, u32[]{:S(2)}) async-start(bf16[128,6,768]{2,1,0:T(8,128)(2,1)} %broadcast_in_dim.22), calls=%async_computation.3 | async-start | bytes 3145728 | tf_op jit(solution)/shard_map/all_to_all | solution.py:342
  163.2 30.3 %copy-start.5 = (bf16[1024,384]{1,0:T(8,128)(2,1)S(1)}, bf16[1024,384]{1,0:T(8,128)(2,1)}, u32[]{:S(2)}) copy-start(bf16[1024,384]{1,0:T(8,128)(2,1)} %get-tuple-element.41) | copy-start | bytes 2359300
  193.5 2.6 %copy-start = (bf16[1024,384]{1,0:T(8,128)(2,1)S(1)}, bf16[1024,384]{1,0:T(8,128)(2,1)}, u32[]{:S(2)}) copy-start(bf16[1024,384]{1,0:T(8,128)(2,1)} %get-tuple-element.37) | copy-start | bytes 2359300
  193.5 2.6 %copy-start.1 = (bf16[1024,384]{1,0:T(8,128)(2,1)S(1)}, bf16[1024,384]{1,0:T(8,128)(2,1)}, u32[]{:S(2)}) copy-start(bf16[1024,384]{1,0:T(8,128)(2,1)} %get-tuple-element.39) | copy-start | bytes 2359300
  193.5 2.6 %copy-start.2 = (bf16[1024,384]{1,0:T(8,128)(2,1)S(1)}, bf16[1024,384]{1,0:T(8,128)(2,1)}, u32[]{:S(2)}) copy-start(bf16[1024,384]{1,0:T(8,128)(2,1)} %get-tuple-element.34) | copy-start | bytes 2359300
  193.5 2.6 %copy-start.3 = (bf16[1024,384]{1,0:T(8,128)(2,1)S(1)}, bf16[1024,384]{1,0:T(8,128)(2,1)}, u32[]{:S(2)}) copy-start(bf16[1024,384]{1,0:T(8,128)(2,1)} %get-tuple-element.38) | copy-start | bytes 2359300

commit v2 on v1

v2 whole, which is shorter than its diff:
```python
import functools

import jax
import jax.numpy as jnp
from jax import lax
from jax.experimental import pallas as pl
from jax.experimental.pallas import tpu as pltpu
from jax.sharding import PartitionSpec as P

HEADS = 16
HEAD = 48
ROWS = 1024
RATE = 16
PICKED = ROWS // RATE
WIDTH = 768
GROUP = 8
COLS = GROUP * HEAD
PACK = 256
CHUNK = 512
STEP = 256
STACK = 4 * HEAD
BACK = 3 * HEAD + 16
PAIR = 2
SAFE = 64.0
SLOT = 8
ROOT = HEAD**-0.5
SCALE = ROOT * 1.4426950408889634
BF = jnp.bfloat16
F32 = jnp.float32
VMEM_LIMIT = 56 << 20


def dot(left, right):
    return lax.dot_general(left, right, (((1,), (0,)), ((), ())), preferred_element_type=F32)


def dot_t(left, right):
    return lax.dot_general(left, right, (((1,), (1,)), ((), ())), preferred_element_type=F32)


def split2(x):
    hi = x.astype(BF)
    return hi, (x - hi.astype(F32)).astype(BF)


def split3(x):
    hi = x.astype(BF)
    rest = x - hi.astype(F32)
    mid = rest.astype(BF)
    return hi.astype(F32), mid.astype(F32), rest - mid.astype(F32)


def rows16(parts):
    which = lax.broadcasted_iota(jnp.int32, (16, parts[0].shape[1]), 0)
    out = jnp.zeros(which.shape, F32)
    for row, part in enumerate(parts):
        out = jnp.where(which == row, part, out)
    return out


def score_operands(query, key, top):
    hi, lo = split2(query.astype(F32) * SCALE)
    pad = jnp.zeros((16, ROWS), BF)
    right = jnp.concatenate([hi, lo, rows16([-top]).astype(BF), pad], axis=0)
    ones = rows16([jnp.ones((1, ROWS), F32)]).astype(BF)
    left = jnp.concatenate([key, key, ones, pad], axis=0).T
    return left, right


def guard(heads, top_ref):
    bounds = []
    for query, key in heads:
        qq, kk = query.astype(F32), key.astype(F32)
        qn = jnp.sum(qq * qq, axis=0, keepdims=True)
        kn = jnp.sum(kk * kk, axis=0, keepdims=True)
        bounds.append(jnp.max(qn) * jnp.max(kn) * (SCALE * SCALE))
    top_ref[...] = jnp.zeros(top_ref.shape, F32)

    @pl.when(functools.reduce(jnp.maximum, bounds) > SAFE * SAFE)
    def _():
        for i, (query, key) in enumerate(heads):
            left, right = score_operands(query, key, jnp.zeros((1, ROWS), F32))
            for start in range(0, ROWS, CHUNK):
                cols = slice(start, start + CHUNK)
                top = jnp.max(dot(left, right[:, cols]), axis=0, keepdims=True)
                top_ref[i, 0:1, cols] = top.astype(BF).astype(F32)


def attend(query, key, value, top, e_ref):
    left, right = score_operands(query, key, top)
    weights = jnp.concatenate([value, jnp.ones((16, ROWS), BF)], axis=0)
    for start in range(0, ROWS, CHUNK):
        cols = slice(start, start + CHUNK)
        e_ref[:, cols] = jnp.exp2(dot(left, right[:, cols])).astype(BF)
    return dot(weights, e_ref[...])


def gradient_operands(value, dattend, ratio, inner):
    hi, lo = split2(dattend * ratio)
    ihi, ilo = split2(-inner * ratio)
    tail = rows16([ihi.astype(F32), ilo.astype(F32)]).astype(BF)
    pad = jnp.zeros((16, ROWS), BF)
    right = jnp.concatenate([hi, lo, tail, pad], axis=0)
    one = jnp.ones((1, ROWS), F32)
    left = jnp.concatenate([value, value, rows16([one, one]).astype(BF), pad], axis=0).T
    return left, right, hi


def gradient_chunks(e_ref, query, key, operands, ds_ref):
    left, right, hi = operands
    starts = range(0, ROWS, STEP)
    def first(start):
        rows = slice(start, start + STEP)
        ds_ref[rows, :] = dot(left[rows, :], right).astype(BF) * e_ref[rows, :]
    dq, dks, dvs = None, [], []
    first(0)
    for start in starts:
        rows = slice(start, start + STEP)
        dvs.append(dot_t(hi, e_ref[rows, :]))
        if start + STEP < ROWS:
            first(start + STEP)
        dks.append(dot_t(query, ds_ref[rows, :]))
        term = dot(key[:, rows], ds_ref[rows, :])
        dq = term if dq is None else dq + term
    return dq * ROOT, jnp.concatenate(dks, axis=1) * ROOT, jnp.concatenate(dvs, axis=1)


def gradients(e_ref, query, key, value, dattend, ratio, inner, ds_ref):
    return gradient_chunks(e_ref, query, key, gradient_operands(value, dattend, ratio, inner), ds_ref)


def prologue_kernel(off_ref, q_ref, k_ref, v_ref, g_ref, w_ref, stack_ref, sel_ref, pack_ref, picked_ref, score_ref, e_ref):
    group = pl.program_id(0)
    dattend = dot_t(w_ref[...], g_ref[...]).astype(BF)
    for i, source in enumerate((q_ref[...].T, k_ref[...].T, v_ref[...].T, dattend)):
        for h in range(GROUP):
            stack_ref[h, i * HEAD : (i + 1) * HEAD, :] = source[h * HEAD : (h + 1) * HEAD]
    row = lax.broadcasted_iota(jnp.int32, (PICKED, ROWS), 0)
    tile = lax.broadcasted_iota(jnp.int32, (PICKED, ROWS), 1) - RATE * row
    for h in range(GROUP):
        pick = jnp.where(tile == off_ref[group * GROUP + h], 1.0, 0.0).astype(BF)
        sel_ref[h] = pick
        picked = dot_t(pick, stack_ref[h]).astype(BF)
        picked_ref[h] = picked
        score_ref[h * PICKED : (h + 1) * PICKED, :] = dot(picked[:, :HEAD], stack_ref[h, HEAD : 2 * HEAD, :])
    score = score_ref[...] * SCALE
    top = jnp.max(score, axis=1, keepdims=True)
    e = jnp.exp2(score - top)
    total = jnp.sum(e, axis=1, keepdims=True)
    e_ref[...] = e.astype(BF)
    lane = lax.broadcasted_iota(jnp.int32, (GROUP * PICKED, PACK), 1)
    scalars = jnp.zeros((GROUP * PICKED, PACK), F32)
    for place, part in enumerate(split3(top) + split3(total)):
        scalars = jnp.where(lane == 5 * HEAD + place, part, scalars)
    recip = 1.0 / total
    spot_row = lax.broadcasted_iota(jnp.int32, (STACK, PACK), 0)
    spot_col = lax.broadcasted_iota(jnp.int32, (STACK, PACK), 1)
    keep = jnp.where(spot_col == spot_row, 1.0, 0.0).astype(BF)
    spot = jnp.where(spot_col == spot_row + STACK, 1.0, 0.0).astype(BF)[:HEAD]
    for h in range(GROUP):
        rows = slice(h * PICKED, (h + 1) * PICKED)
        near = dot_t(e_ref[rows, :], stack_ref[h, 2 * HEAD : 3 * HEAD, :]) * recip[rows]
        pack_ref[h] = (dot(picked_ref[h], keep) + dot(near.astype(BF), spot) + scalars[rows]).astype(BF)


def part(ref, i, which):
    return ref[i, which * HEAD : (which + 1) * HEAD, :]


def forward_kernel(stack_ref, *refs):
    e_ref, att_ref, stat_ref, top_ref = refs[-4:]
    guard([(part(stack_ref, i, 0), part(stack_ref, i, 1)) for i in range(PAIR)], top_ref)
    for i in range(PAIR):
        top = top_ref[i, 0:1, :]
        sums = attend(part(stack_ref, i, 0), part(stack_ref, i, 1), part(stack_ref, i, 2), top, e_ref.at[i])
        recip = 1.0 / sums[HEAD : HEAD + 1, :]
        att_ref[i * HEAD : (i + 1) * HEAD, :] = (sums[:HEAD, :] * recip).astype(BF)
        stat_ref[i, 0:1, :] = top
        stat_ref[i, 1:2, :] = recip


def far_kernel(in_ref, out_ref, e_ref, ds_ref, top_ref):
    packed = in_ref[...].T
    query, key, value = (packed[i * HEAD : (i + 1) * HEAD] for i in range(3))
    dattend = packed[3 * HEAD : 4 * HEAD].astype(F32)
    near_att = packed[4 * HEAD : 5 * HEAD].astype(F32)
    tail = packed[5 * HEAD :].astype(F32)
    near_top = tail[0:1] + tail[1:2] + tail[2:3]
    near_total = tail[3:4] + tail[4:5] + tail[5:6]
    guard([(query, key)], top_ref)
    far_top = top_ref[0, 0:1, :]
    sums = attend(query, key, value, far_top, e_ref)
    top = jnp.maximum(near_top, far_top)
    near_part = near_total * jnp.exp2(near_top - top)
    far_scale = jnp.exp2(far_top - top)
    total = near_part + sums[HEAD : HEAD + 1, :] * far_scale
    recip = 1.0 / total
    att = ((near_att * near_part + sums[:HEAD, :] * far_scale) * recip).astype(BF)
    inner = jnp.sum(att.astype(F32) * dattend, axis=0, keepdims=True)
    dq, dk, dv = gradients(e_ref, query, key, value, dattend, far_scale * recip, inner, ds_ref)
    scalars = rows16(split3(top + jnp.log2(total)) + split3(inner)).astype(BF)
    back = jnp.concatenate(
        [dq.astype(BF), dk.astype(BF), dv.astype(BF), scalars, att, jnp.zeros((PACK - BACK - HEAD, ROWS), BF)], axis=0
    )
    out_ref[...] = back.T


def output_kernel(off_ref, att_ref, sel_ref, back_ref, w_ref, g_ref, out_ref, wg_ref, full_ref, acc_ref):
    group = pl.program_id(0)
    tile = lax.broadcasted_iota(jnp.int32, (HEAD, ROWS), 1) % RATE
    for h in range(GROUP):
        rows = slice(h * HEAD, (h + 1) * HEAD)
        placed = dot(back_ref[h].T[BACK : BACK + HEAD], sel_ref[h]).astype(BF)
        full_ref[rows, :] = jnp.where(tile == off_ref[group * GROUP + h], placed, att_ref[rows, :])
    att = full_ref[...]
    wg_ref[0, : COLS // SLOT] = dot(att, g_ref[...]).reshape(COLS // SLOT, SLOT, WIDTH).astype(BF)
    wg_ref[0, COLS // SLOT :] = jnp.zeros((wg_ref.shape[1] - COLS // SLOT, SLOT, WIDTH), BF)
    term = dot(att.T, w_ref[...])

    @pl.when(group == 0)
    def _():
        acc_ref[...] = term

    @pl.when(group == pl.num_programs(0) - 1)
    def _():
        out_ref[...] = (acc_ref[...] + term).astype(BF)


def backward_kernel(first, off_ref, e_ref, stack_ref, sel_ref, att_ref, stat_ref, back_ref, *refs):
    dq_ref, dk_ref, dv_ref, ds_ref, tq_ref, tk_ref, tv_ref = refs[-7:]
    step = pl.program_id(1)
    ready = []
    for i in range(PAIR):
        h = step * PAIR + i
        offset = off_ref[first + pl.program_id(0) * GROUP + h]
        placed = dot(back_ref[i].T[:BACK], sel_ref[i])
        tail = placed[3 * HEAD : 3 * HEAD + 8]
        joint = tail[0:1] + tail[1:2] + tail[2:3]
        far_inner = tail[3:4] + tail[4:5] + tail[5:6]
        dilated = lax.broadcasted_iota(jnp.int32, (1, ROWS), 1) % RATE == offset
        dattend = part(stack_ref, i, 3).astype(F32)
        ratio = jnp.where(dilated, jnp.exp2(jnp.where(dilated, stat_ref[i, 0:1, :] - joint, 0.0)), stat_ref[i, 1:2, :])
        inner = jnp.sum(dattend * att_ref[i * HEAD : (i + 1) * HEAD, :].astype(F32), axis=0, keepdims=True)
        inner = jnp.where(dilated, far_inner, inner)
        ready.append((placed, gradient_operands(part(stack_ref, i, 2), dattend, ratio, inner)))
    for i, (placed, operands) in enumerate(ready):
        h = step * PAIR + i
        dq, dk, dv = gradient_chunks(e_ref.at[i], part(stack_ref, i, 0), part(stack_ref, i, 1), operands, ds_ref.at[i])
        rows = pl.ds(pl.multiple_of(h * HEAD, 16), HEAD)
        tq_ref[rows, :] = (dq + placed[:HEAD]).astype(BF)
        tk_ref[rows, :] = (dk + placed[HEAD : 2 * HEAD]).astype(BF)
        tv_ref[rows, :] = (dv + placed[2 * HEAD : 3 * HEAD]).astype(BF)

    @pl.when(step == pl.num_programs(1) - 1)
    def _():
        dq_ref[...] = tq_ref[...].T
        dk_ref[...] = tk_ref[...].T
        dv_ref[...] = tv_ref[...].T


def params():
    return pltpu.CompilerParams(vmem_limit_bytes=VMEM_LIMIT)


def cost(flops, moved, exps=0):
    return pl.CostEstimate(flops=flops, bytes_accessed=moved, transcendentals=exps)


HEAD_FLOPS = 2 * ROWS * ROWS * 256


def prologue(offsets, q, k, v, g, w):
    nat = pl.BlockSpec((ROWS, COLS), lambda i, o: (0, i))
    per_head = lambda rows, cols: pl.BlockSpec((GROUP, rows, cols), lambda i, o: (i, 0, 0))
    return pl.pallas_call(
        prologue_kernel,
        grid_spec=pltpu.PrefetchScalarGridSpec(
            num_scalar_prefetch=1,
            grid=(HEADS // GROUP,),
            in_specs=[nat, nat, nat, pl.BlockSpec((ROWS, WIDTH), lambda i, o: (0, 0)), pl.BlockSpec((COLS, WIDTH), lambda i, o: (i, 0))],
            out_specs=[per_head(STACK, ROWS), per_head(PICKED, ROWS), per_head(PICKED, PACK)],
            scratch_shapes=[
                pltpu.VMEM((GROUP, PICKED, STACK), BF),
                pltpu.VMEM((GROUP * PICKED, ROWS), F32),
                pltpu.VMEM((GROUP * PICKED, ROWS), BF),
            ],
        ),
        out_shape=[
            jax.ShapeDtypeStruct((HEADS, STACK, ROWS), BF),
            jax.ShapeDtypeStruct((HEADS, PICKED, ROWS), BF),
            jax.ShapeDtypeStruct((HEADS, PICKED, PACK), BF),
        ],
        compiler_params=params(),
        cost_estimate=cost(4 * HEAD_FLOPS, 14 << 20, 1 << 20),
        name="prologue",
    )(offsets, q, k, v, g, w)


def forward(stack, first, count, before=None):
    carried = [] if before is None else [before]
    return pl.pallas_call(
        forward_kernel,
        grid=(count // PAIR,),
        in_specs=[pl.BlockSpec((PAIR, STACK, ROWS), lambda i: (i + first // PAIR, 0, 0))]
        + [pl.BlockSpec(memory_space=pl.ANY)] * len(carried),
        out_specs=[
            pl.BlockSpec((PAIR, ROWS, ROWS), lambda i: (i, 0, 0)),
            pl.BlockSpec((PAIR * HEAD, ROWS), lambda i: (i + first // PAIR, 0)),
            pl.BlockSpec((PAIR, 8, ROWS), lambda i: (i, 0, 0)),
        ],
        out_shape=[
            jax.ShapeDtypeStruct((count, ROWS, ROWS), BF),
            jax.ShapeDtypeStruct((WIDTH, ROWS), BF),
            jax.ShapeDtypeStruct((count, 8, ROWS), F32),
        ],
        scratch_shapes=[pltpu.VMEM((PAIR, 8, ROWS), F32)],
        input_output_aliases={1: 1} if carried else {},
        compiler_params=params(),
        cost_estimate=cost(2 * count * HEAD_FLOPS, count * (2 << 20), count << 20),
        name="near_forward",
    )(stack, *carried)


def far(packed):
    return pl.pallas_call(
        far_kernel,
        out_shape=jax.ShapeDtypeStruct((ROWS, PACK), BF),
        scratch_shapes=[pltpu.VMEM((ROWS, ROWS), BF), pltpu.VMEM((ROWS, ROWS), BF), pltpu.VMEM((1, 8, ROWS), F32)],
        compiler_params=params(),
        cost_estimate=cost(6 * HEAD_FLOPS, 1 << 20, 1 << 20),
        name="far",
    )(packed)


def project(offsets, att, sel, back, w, g, devices):
    groups = HEADS // GROUP
    return pl.pallas_call(
        output_kernel,
        grid_spec=pltpu.PrefetchScalarGridSpec(
            num_scalar_prefetch=1,
            grid=(groups,),
            in_specs=[
                pl.BlockSpec((COLS, ROWS), lambda i, o: (i, 0)),
                pl.BlockSpec((GROUP, PICKED, ROWS), lambda i, o: (i, 0, 0)),
                pl.BlockSpec((GROUP, PICKED, PACK), lambda i, o: (i, 0, 0)),
                pl.BlockSpec((COLS, WIDTH), lambda i, o: (i, 0)),
                pl.BlockSpec((ROWS, WIDTH), lambda i, o: (0, 0)),
            ],
            out_specs=[
                pl.BlockSpec((ROWS, WIDTH), lambda i, o: (0, 0)),
                pl.BlockSpec((1, devices // groups, SLOT, WIDTH), lambda i, o: (i, 0, 0, 0)),
            ],
            scratch_shapes=[pltpu.VMEM((COLS, ROWS), BF), pltpu.VMEM((ROWS, WIDTH), F32)],
        ),
        out_shape=[
            jax.ShapeDtypeStruct((ROWS, WIDTH), BF),
            jax.ShapeDtypeStruct((groups, devices // groups, SLOT, WIDTH), BF),
        ],
        compiler_params=params(),
        cost_estimate=cost(4 * ROWS * WIDTH * WIDTH, 10 << 20),
        name="project",
    )(offsets, att, sel, back, w, g)


def backward(offsets, e, stack, sel, att, stat, back, first, count, before=()):
    start, steps = first // PAIR, GROUP // PAIR
    out = pl.BlockSpec((ROWS, COLS), lambda g, h, o: (0, first // GROUP + g))
    whole = lambda rows, cols: pl.BlockSpec((PAIR, rows, cols), lambda g, h, o: (start + g * steps + h, 0, 0))
    piece = lambda rows, cols: pl.BlockSpec((PAIR, rows, cols), lambda g, h, o: (g * steps + h, 0, 0))
    return pl.pallas_call(
        functools.partial(backward_kernel, first),
        grid_spec=pltpu.PrefetchScalarGridSpec(
            num_scalar_prefetch=1,
            grid=(count // GROUP, steps),
            in_specs=[
                piece(ROWS, ROWS),
                whole(STACK, ROWS),
                whole(PICKED, ROWS),
                pl.BlockSpec((PAIR * HEAD, ROWS), lambda g, h, o: (start + g * steps + h, 0)),
                piece(8, ROWS),
                whole(PICKED, PACK),
            ]
            + [pl.BlockSpec(memory_space=pl.ANY)] * len(before),
            out_specs=[out] * 3,
            scratch_shapes=[pltpu.VMEM((PAIR, ROWS, ROWS), BF)] + [pltpu.VMEM((COLS, ROWS), BF)] * 3,
        ),
        out_shape=[jax.ShapeDtypeStruct((ROWS, WIDTH), BF)] * 3,
        input_output_aliases={7 + i: i for i in range(len(before))},
        compiler_params=params(),
        cost_estimate=cost(4 * count * HEAD_FLOPS, count * (2 << 20)),
        name="near_backward",
    )(offsets, e, stack, sel, att, stat, back, *before)


def body(queries, keys, values, offsets, w_out, grad_out):
    upstream = grad_out[0]
    stack, sel, packed = prologue(offsets, queries[0], keys[0], values[0], upstream, w_out)
    arrived = lax.all_to_all(packed, "ctx", 0, 0, tiled=True)
    half = HEADS // 2
    e0, att, stat0 = forward(stack, 0, half)
    far_out = far(arrived.reshape(ROWS, PACK)).reshape(HEADS, PICKED, PACK)
    back = lax.all_to_all(far_out, "ctx", 0, 0, tiled=True)
    e1, att, stat1 = forward(stack, half, half, att)
    devices = lax.axis_size("dp") * lax.axis_size("ctx")
    output, weight_part = project(offsets, att, sel, back, w_out, upstream, devices)
    pieces = lax.all_to_all(weight_part.reshape(devices, SLOT, WIDTH), ("dp", "ctx"), 0, 0, tiled=True)
    grads = backward(offsets, e0, stack, sel, att, stat0, back, 0, half)
    total = jnp.sum(pieces.astype(F32), axis=0).astype(BF)
    whole = lax.all_to_all(jnp.broadcast_to(total[None], pieces.shape), ("dp", "ctx"), 0, 0, tiled=True)
    dq, dk, dv = backward(offsets, e1, stack, sel, att, stat1, back, half, half, grads)
    groups = HEADS // GROUP
    whole = whole.reshape(groups, devices // groups, SLOT, WIDTH)[:, : COLS // SLOT].reshape(WIDTH, WIDTH)
    weight_grad = whole.astype(F32) * (ROWS * devices) ** -0.5
    return output[None], dq[None], dk[None], dv[None], weight_grad


def solution(mesh):
    rows = P("dp", "ctx", None)
    return jax.shard_map(
        body,
        mesh=mesh,
        in_specs=(rows, rows, rows, P(), P(), rows),
        out_specs=(rows, rows, rows, rows, P()),
        check_vma=False,
    )
```

time: 202 us -> 153 us (0.76)
  Pallas kernels: 147 us -> 109 us
  other arithmetic: 9 us -> 1.89 us
  local copies, waits for them, and re-layouts: 8.29 us -> 2.9 us
  waiting for transfers between devices: 0.01 us -> 3.92 us
  starting transfers between devices: 36.1 us -> 33.7 us
    pallas_call x4, Pallas kernels: 113 us -> 79 us  [the longest x2 45.6 us: backward(): pl.pallas_call(functools.partial(backward_kernel, first), grid_spec=pltpu...]
    broadcast_in_dim x2 -> x0, other arithmetic: 4.46 us -> none  [body(): return (output[None], dq[None], dk[None], dv[None], weight_grad)]
    reshape x1 -> x0, local copies, waits for them, and re-layouts: 3.19 us -> none  [body(): weight_part.reshape(devices, WIDTH // devices, WIDTH)]
    pallas_call x1, Pallas kernels: 17.9 us -> 15.1 us  [prologue(): pl.pallas_call(prologue_kernel, grid_spec=pltpu.PrefetchScalarGridSpec(nu...]
    concatenate x1 -> x0, other arithmetic: 2.4 us -> none  [body(): jnp.concatenate([att0, att1], axis=0)]
    all_to_all x1, starting transfers between devices: 10.2 us -> 7.79 us  [body(): lax.all_to_all(jnp.broadcast_to(total[None], pieces.shape), ('dp', 'ctx')...]
  transfers between devices with their start and end apart: 4 -> 4, of which waited for: 0 -> 2; matrix products, arithmetic and copies ran while one was open for 4% -> 0% of each run, Pallas kernels for 56% -> 52%
where the time goes in v2:
time: 153 us; the launch traced here: 152 us
  Pallas kernels  109 us (71%)
  starting transfers between devices  33.7 us (22%)
  waiting for transfers between devices  3.92 us (3%)
  local copies, waits for them, and re-layouts  2.9 us (2%)
  other arithmetic  1.89 us (1%)
    pallas_call x2, Pallas kernels, backward(): pl.pallas_call(functools.partial(backward_kernel, first), grid_spec=pltpu...  45.6 us
    pallas_call x2, Pallas kernels, forward(): pl.pallas_call(forward_kernel, grid=(count // PAIR,), in_specs=[pl.BlockS...  33.4 us
    pallas_call x1, Pallas kernels, prologue(): pl.pallas_call(prologue_kernel, grid_spec=pltpu.PrefetchScalarGridSpec(nu...  15.1 us
    all_to_all x1, starting transfers between devices, body(): lax.all_to_all(weight_part.reshape(devices, SLOT, WIDTH), ('dp', 'ctx'),...  9.43 us
    all_to_all x1, starting transfers between devices, body(): arrived = lax.all_to_all(packed, 'ctx', 0, 0, tiled=True)  9.29 us
    pallas_call x1, Pallas kernels, project(): pl.pallas_call(output_kernel, grid_spec=pltpu.PrefetchScalarGridSpec(num_...  8.94 us
    all_to_all x1, starting transfers between devices, body(): lax.all_to_all(jnp.broadcast_to(total[None], pieces.shape), ('dp', 'ctx')...  7.79 us
    all_to_all x1, starting transfers between devices, body(): back = lax.all_to_all(far_out, 'ctx', 0, 0, tiled=True)  7.23 us
  transfers between devices with their start and end apart: 4, of which 2 were waited for; matrix products, arithmetic and copies ran while one was open for 0% of the time, Pallas kernels for 52%

profile of v2, /device:TPU:1, one launch (start us, length us, event | category | flops | bytes accessed | tf_op | source)
XLA Modules:
  0.0 152.1 jit_solution(7708639898618370604)
XLA Ops:
  0.6 15.1 %prologue.1 = (bf16[16,192,1024]{2,1,0:T(8,128)(2,1)}, bf16[16,64,1024]{2,1,0:T(8,128)(2,1)}, bf16[16,64,256]{2,1,0:T(8,128)(2,1)}) custom-call(s32[16]{0:T(128)} %off_ref.7, bf16[1024,768]{1,0:T(8,128)(2,1)} %bitcast.18, bf16[1024,768]{1,0:T(8,128)(2,1)} %bitcast.19, bf16[1024,768]{1,0:T(8,128)(2,1)} %bitcast.20, bf16[1024,768]{1,0:T(8,128)(2,1)} %bitcast.21, ...), custom_call_target="tpu_custom_call" | custom-call | flops 2147483648 | bytes 14680064 | tf_op jit(solution)/shard_map/prologue/pallas_call | solution.py:275
  15.7 9.3 %all-to-all-start = ((bf16[16,64,256]{2,1,0:T(8,128)(2,1)}), bf16[16,64,256]{2,1,0:T(8,128)(2,1)S(1)}, u32[]{:S(2)}, u32[]{:S(2)}) async-start(bf16[16,64,256]{2,1,0:T(8,128)(2,1)} %get-tuple-element.26), calls=%async_computation | async-start | bytes 1048576 | tf_op jit(solution)/shard_map/all_to_all | solution.py:398
  25.0 16.7 %near_forward.2 = (bf16[8,1024,1024]{2,1,0:T(8,128)(2,1)}, bf16[768,1024]{1,0:T(8,128)(2,1)}, f32[8,8,1024]{2,1,0:T(8,128)}) custom-call(bf16[16,192,1024]{2,1,0:T(8,128)(2,1)} %get-tuple-element.22.stack_ref), custom_call_target="tpu_custom_call" | custom-call | flops 8589934592 | bytes 16777216 | tf_op jit(solution)/shard_map/near_forward/pallas_call | solution.py:301
  41.7 0.0 all-to-all-done
  41.7 0.0 copy-start.1
  41.7 0.8 copy-done.1
  42.5 6.0 %far.1 = bf16[1024,256]{1,0:T(8,128)(2,1)} custom-call(bf16[1024,256]{1,0:T(8,128)(2,1)} %bitcast.16), custom_call_target="tpu_custom_call" | custom-call | flops 3221225472 | bytes 1048576 | tf_op jit(solution)/shard_map/far/pallas_call | solution.py:325
  48.5 7.2 %all-to-all-start.1 = ((bf16[16,64,256]{2,1,0:T(8,128)(2,1)}), bf16[16,64,256]{2,1,0:T(8,128)(2,1)S(1)}, u32[]{:S(2)}, u32[]{:S(2)}) async-start(bf16[16,64,256]{2,1,0:T(8,128)(2,1)} %bitcast.17), calls=%async_computation.1 | async-start | bytes 1048576 | tf_op jit(solution)/shard_map/all_to_all | solution.py:402
  55.7 16.7 %near_forward.3 = (bf16[8,1024,1024]{2,1,0:T(8,128)(2,1)}, bf16[768,1024]{1,0:T(8,128)(2,1)}, f32[8,8,1024]{2,1,0:T(8,128)}) custom-call(bf16[16,192,1024]{2,1,0:T(8,128)(2,1)} %get-tuple-element.22.stack_ref, bf16[768,1024]{1,0:T(8,128)(2,1)} %get-tuple-element.23.refs_0_), custom_call_target="tpu_custom_call", output_to_operand_aliasing={{1}: (1, {})} | custom-call | flops 8589934592 | bytes 16777216 | tf_op jit(solution)/shard_map/near_forward/pallas_call | solution.py:301
  72.4 0.0 all-to-all-done.1.back_ref
  72.4 0.0 copy-start
  72.4 0.8 copy-done
  73.3 8.9 %project.1 = (bf16[1024,768]{1,0:T(8,128)(2,1)}, bf16[2,64,8,768]{3,2,1,0:T(8,128)(2,1)}) custom-call(s32[16]{0:T(128)} %off_ref.7, bf16[768,1024]{1,0:T(8,128)(2,1)} %get-tuple-element.24.att_ref, bf16[16,64,1024]{2,1,0:T(8,128)(2,1)} %get-tuple-element.25.sel_ref, bf16[16,64,256]{2,1,0:T(8,128)(2,1)} %copy-done, bf16[768,768]{1,0:T(8,128)(2,1)} %w_ref.3, ...), custom_call_target="tpu_custom_call" | custom-call | flops 2415919104 | bytes 10485760 | tf_op jit(solution)/shard_map/project/pallas_call | solution.py:337
  82.2 9.4 %all-to-all-start.2 = ((bf16[128,8,768]{2,1,0:T(8,128)(2,1)}), bf16[128,8,768]{2,1,0:T(8,128)(2,1)S(1)}, u32[]{:S(2)}, u32[]{:S(2)}) async-start(bf16[128,8,768]{2,1,0:T(8,128)(2,1)} %bitcast.15), calls=%async_computation.2 | async-start | bytes 3145728 | tf_op jit(solution)/shard_map/all_to_all | solution.py:406
  91.6 22.8 %near_backward.2 = (bf16[1024,768]{1,0:T(8,128)(2,1)}, bf16[1024,768]{1,0:T(8,128)(2,1)}, bf16[1024,768]{1,0:T(8,128)(2,1)}) custom-call(s32[16]{0:T(128)} %off_ref.7, bf16[8,1024,1024]{2,1,0:T(8,128)(2,1)} %get-tuple-element.30.e_ref, bf16[16,192,1024]{2,1,0:T(8,128)(2,1)} %get-tuple-element.22.stack_ref, bf16[16,64,1024]{2,1,0:T(8,128)(2,1)} %get-tuple-element.25.sel_ref, ...), custom_call_target="tpu_custom_call" | custom-call | flops 17179869184 | bytes 16777216 | tf_op jit(solution)/shard_map/near_backward/pallas_call | solution.py:370
  114.4 2.0 %all-to-all-done.2 = bf16[128,8,768]{2,1,0:T(8,128)(2,1)S(1)} async-done(((bf16[128,8,768]{2,1,0:T(8,128)(2,1)}), bf16[128,8,768]{2,1,0:T(8,128)(2,1)S(1)}, u32[]{:S(2)}, u32[]{:S(2)}) %all-to-all-start.2) | async-done | bytes 1572896 | tf_op jit(solution)/shard_map/all_to_all | solution.py:406
  116.4 0.3 reduce_sum.12
  116.7 1.3 broadcast_in_dim.22
  118.0 7.8 %all-to-all-start.3 = ((bf16[128,8,768]{2,1,0:T(8,128)(2,1)}), bf16[128,8,768]{2,1,0:T(8,128)(2,1)S(1)}, u32[]{:S(2)}, u32[]{:S(2)}) async-start(bf16[128,8,768]{2,1,0:T(8,128)(2,1)} %broadcast_in_dim.22), calls=%async_computation.3 | async-start | bytes 3145728 | tf_op jit(solution)/shard_map/all_to_all | solution.py:409
  125.8 22.8 %near_backward.3 = (bf16[1024,768]{1,0:T(8,128)(2,1)}, bf16[1024,768]{1,0:T(8,128)(2,1)}, bf16[1024,768]{1,0:T(8,128)(2,1)}) custom-call(s32[16]{0:T(128)} %off_ref.7, bf16[8,1024,1024]{2,1,0:T(8,128)(2,1)} %get-tuple-element.28.e_ref, ...), custom_call_target="tpu_custom_call", output_to_operand_aliasing={{0}: (7, {}), {1}: (8, {}), {2}: (9, {})} | custom-call | flops 17179869184 | bytes 16777216 | tf_op jit(solution)/shard_map/near_backward/pallas_call | solution.py:370
  148.6 1.9 %all-to-all-done.3 = bf16[128,8,768]{2,1,0:T(8,128)(2,1)S(1)} async-done(((bf16[128,8,768]{2,1,0:T(8,128)(2,1)}), bf16[128,8,768]{2,1,0:T(8,128)(2,1)S(1)}, u32[]{:S(2)}, u32[]{:S(2)}) %all-to-all-start.3) | async-done | bytes 1572896 | tf_op jit(solution)/shard_map/all_to_all | solution.py:409
  150.5 1.6 %convert_multiply_fusion = f32[2,48,8,768]{3,2,1,0:T(8,128)} fusion(bf16[2,64,8,768]{3,2,1,0:T(8,128)(2,1)S(1)} %bitcast.13), kind=kLoop, calls=%fused_computation | loop fusion | flops 1179648 | bytes 3538944 | tf_op jit(solution)/shard_map/mul | solution.py:413
Async XLA Ops:
  15.7 26.0 %all-to-all-start = ((bf16[16,64,256]{2,1,0:T(8,128)(2,1)}), bf16[16,64,256]{2,1,0:T(8,128)(2,1)S(1)}, u32[]{:S(2)}, u32[]{:S(2)}) async-start(bf16[16,64,256]{2,1,0:T(8,128)(2,1)} %get-tuple-element.26), calls=%async_computation | async-start | bytes 1048576 | tf_op jit(solution)/shard_map/all_to_all | solution.py:398
  41.7 0.8 copy-start.1
  48.5 23.9 %all-to-all-start.1 = ((bf16[16,64,256]{2,1,0:T(8,128)(2,1)}), bf16[16,64,256]{2,1,0:T(8,128)(2,1)S(1)}, u32[]{:S(2)}, u32[]{:S(2)}) async-start(bf16[16,64,256]{2,1,0:T(8,128)(2,1)} %bitcast.17), calls=%async_computation.1 | async-start | bytes 1048576 | tf_op jit(solution)/shard_map/all_to_all | solution.py:402
  72.4 0.8 copy-start
  82.2 34.2 %all-to-all-start.2 = ((bf16[128,8,768]{2,1,0:T(8,128)(2,1)}), bf16[128,8,768]{2,1,0:T(8,128)(2,1)S(1)}, u32[]{:S(2)}, u32[]{:S(2)}) async-start(bf16[128,8,768]{2,1,0:T(8,128)(2,1)} %bitcast.15), calls=%async_computation.2 | async-start | bytes 3145728 | tf_op jit(solution)/shard_map/all_to_all | solution.py:406
  118.0 32.6 %all-to-all-start.3 = ((bf16[128,8,768]{2,1,0:T(8,128)(2,1)}), bf16[128,8,768]{2,1,0:T(8,128)(2,1)S(1)}, u32[]{:S(2)}, u32[]{:S(2)}) async-start(bf16[128,8,768]{2,1,0:T(8,128)(2,1)} %broadcast_in_dim.22), calls=%async_computation.3 | async-start | bytes 3145728 | tf_op jit(solution)/shard_map/all_to_all | solution.py:409

commit v3 on v2

--- a/solution.py
+++ b/solution.py
@@ -67,16 +67,17 @@
     return left, right
 
 
-def guard(heads, top_ref):
-    bounds = []
-    for query, key in heads:
-        qq, kk = query.astype(F32), key.astype(F32)
-        qn = jnp.sum(qq * qq, axis=0, keepdims=True)
-        kn = jnp.sum(kk * kk, axis=0, keepdims=True)
-        bounds.append(jnp.max(qn) * jnp.max(kn) * (SCALE * SCALE))
+def squared_bound(query, key):
+    qq, kk = query.astype(F32), key.astype(F32)
+    qn = jnp.max(jnp.sum(qq * qq, axis=0, keepdims=True), axis=1, keepdims=True)
+    kn = jnp.max(jnp.sum(kk * kk, axis=0, keepdims=True), axis=1, keepdims=True)
+    return qn * kn * (SCALE * SCALE)
+
+
+def guard(bound, heads, top_ref):
     top_ref[...] = jnp.zeros(top_ref.shape, F32)
 
-    @pl.when(functools.reduce(jnp.maximum, bounds) > SAFE * SAFE)
+    @pl.when(jnp.logical_not(bound <= SAFE * SAFE))
     def _():
         for i, (query, key) in enumerate(heads):
             left, right = score_operands(query, key, jnp.zeros((1, ROWS), F32))
@@ -113,23 +114,24 @@
         rows = slice(start, start + STEP)
         ds_ref[rows, :] = dot(left[rows, :], right).astype(BF) * e_ref[rows, :]
     dq, dks, dvs = None, [], []
+    query_rows = query.T
     first(0)
     for start in starts:
         rows = slice(start, start + STEP)
         dvs.append(dot_t(hi, e_ref[rows, :]))
         if start + STEP < ROWS:
             first(start + STEP)
-        dks.append(dot_t(query, ds_ref[rows, :]))
+        dks.append(dot(ds_ref[rows, :], query_rows))
         term = dot(key[:, rows], ds_ref[rows, :])
         dq = term if dq is None else dq + term
-    return dq * ROOT, jnp.concatenate(dks, axis=1) * ROOT, jnp.concatenate(dvs, axis=1)
+    return dq * ROOT, jnp.concatenate(dks, axis=0).T * ROOT, jnp.concatenate(dvs, axis=1)
 
 
 def gradients(e_ref, query, key, value, dattend, ratio, inner, ds_ref):
     return gradient_chunks(e_ref, query, key, gradient_operands(value, dattend, ratio, inner), ds_ref)
 
 
-def prologue_kernel(off_ref, q_ref, k_ref, v_ref, g_ref, w_ref, stack_ref, sel_ref, pack_ref, picked_ref, score_ref, e_ref):
+def prologue_kernel(off_ref, q_ref, k_ref, v_ref, g_ref, w_ref, stack_ref, sel_ref, pack_ref, bound_ref, picked_ref, score_ref, e_ref):
     group = pl.program_id(0)
     dattend = dot_t(w_ref[...], g_ref[...]).astype(BF)
     for i, source in enumerate((q_ref[...].T, k_ref[...].T, v_ref[...].T, dattend)):
@@ -140,9 +142,12 @@
     for h in range(GROUP):
         pick = jnp.where(tile == off_ref[group * GROUP + h], 1.0, 0.0).astype(BF)
         sel_ref[h] = pick
-        picked = dot_t(pick, stack_ref[h]).astype(BF)
-        picked_ref[h] = picked
-        score_ref[h * PICKED : (h + 1) * PICKED, :] = dot(picked[:, :HEAD], stack_ref[h, HEAD : 2 * HEAD, :])
+        picked_ref[h] = dot_t(pick, stack_ref[h]).astype(BF)
+    for h in range(GROUP):
+        score_ref[h * PICKED : (h + 1) * PICKED, :] = dot(picked_ref[h, :, :HEAD], stack_ref[h, HEAD : 2 * HEAD, :])
+    for h in range(GROUP):
+        bound = squared_bound(stack_ref[h, :HEAD, :], stack_ref[h, HEAD : 2 * HEAD, :])
+        bound_ref[0, h : h + 1, :] = jnp.broadcast_to(bound, (1, 128))
     score = score_ref[...] * SCALE
     top = jnp.max(score, axis=1, keepdims=True)
     e = jnp.exp2(score - top)
@@ -157,19 +162,24 @@
     spot_col = lax.broadcasted_iota(jnp.int32, (STACK, PACK), 1)
     keep = jnp.where(spot_col == spot_row, 1.0, 0.0).astype(BF)
     spot = jnp.where(spot_col == spot_row + STACK, 1.0, 0.0).astype(BF)[:HEAD]
+    nears = []
     for h in range(GROUP):
         rows = slice(h * PICKED, (h + 1) * PICKED)
-        near = dot_t(e_ref[rows, :], stack_ref[h, 2 * HEAD : 3 * HEAD, :]) * recip[rows]
-        pack_ref[h] = (dot(picked_ref[h], keep) + dot(near.astype(BF), spot) + scalars[rows]).astype(BF)
+        nears.append(dot_t(e_ref[rows, :], stack_ref[h, 2 * HEAD : 3 * HEAD, :]) * recip[rows])
+    for h in range(GROUP):
+        rows = slice(h * PICKED, (h + 1) * PICKED)
+        pack_ref[h] = (dot(picked_ref[h], keep) + dot(nears[h].astype(BF), spot) + scalars[rows]).astype(BF)
 
 
 def part(ref, i, which):
     return ref[i, which * HEAD : (which + 1) * HEAD, :]
 
 
-def forward_kernel(stack_ref, *refs):
+def forward_kernel(first, stack_ref, bound_ref, *refs):
     e_ref, att_ref, stat_ref, top_ref = refs[-4:]
-    guard([(part(stack_ref, i, 0), part(stack_ref, i, 1)) for i in range(PAIR)], top_ref)
+    heads = [first + pl.program_id(0) * PAIR + i for i in range(PAIR)]
+    bound = functools.reduce(jnp.maximum, [bound_ref[h // GROUP, h % GROUP, 0] for h in heads])
+    guard(bound, [(part(stack_ref, i, 0), part(stack_ref, i, 1)) for i in range(PAIR)], top_ref)
     for i in range(PAIR):
         top = top_ref[i, 0:1, :]
         sums = attend(part(stack_ref, i, 0), part(stack_ref, i, 1), part(stack_ref, i, 2), top, e_ref.at[i])
@@ -187,7 +197,7 @@
     tail = packed[5 * HEAD :].astype(F32)
     near_top = tail[0:1] + tail[1:2] + tail[2:3]
     near_total = tail[3:4] + tail[4:5] + tail[5:6]
-    guard([(query, key)], top_ref)
+    guard(jnp.max(squared_bound(query, key)), [(query, key)], top_ref)
     far_top = top_ref[0, 0:1, :]
     sums = attend(query, key, value, far_top, e_ref)
     top = jnp.maximum(near_top, far_top)
@@ -205,25 +215,25 @@
     out_ref[...] = back.T
 
 
-def output_kernel(off_ref, att_ref, sel_ref, back_ref, w_ref, g_ref, out_ref, wg_ref, full_ref, acc_ref):
+def output_kernel(off_ref, att_ref, sel_ref, back_ref, w_ref, g_ref, out_ref, wg_ref, full_ref, turned_ref):
     group = pl.program_id(0)
     tile = lax.broadcasted_iota(jnp.int32, (HEAD, ROWS), 1) % RATE
     for h in range(GROUP):
         rows = slice(h * HEAD, (h + 1) * HEAD)
-        placed = dot(back_ref[h].T[BACK : BACK + HEAD], sel_ref[h]).astype(BF)
+        placed = dot(back_ref[group * GROUP + h].T[BACK : BACK + HEAD], sel_ref[h]).astype(BF)
         full_ref[rows, :] = jnp.where(tile == off_ref[group * GROUP + h], placed, att_ref[rows, :])
     att = full_ref[...]
     wg_ref[0, : COLS // SLOT] = dot(att, g_ref[...]).reshape(COLS // SLOT, SLOT, WIDTH).astype(BF)
     wg_ref[0, COLS // SLOT :] = jnp.zeros((wg_ref.shape[1] - COLS // SLOT, SLOT, WIDTH), BF)
-    term = dot(att.T, w_ref[...])
-
-    @pl.when(group == 0)
-    def _():
-        acc_ref[...] = term
+    for g in range(HEADS // GROUP):
+
+        @pl.when(group == g)
+        def _():
+            turned_ref[:, g * COLS : (g + 1) * COLS] = full_ref[...].T
 
     @pl.when(group == pl.num_programs(0) - 1)
     def _():
-        out_ref[...] = (acc_ref[...] + term).astype(BF)
+        out_ref[...] = dot(turned_ref[...], w_ref[...]).astype(BF)
 
 
 def backward_kernel(first, off_ref, e_ref, stack_ref, sel_ref, att_ref, stat_ref, back_ref, *refs):
@@ -233,7 +243,7 @@
     for i in range(PAIR):
         h = step * PAIR + i
         offset = off_ref[first + pl.program_id(0) * GROUP + h]
-        placed = dot(back_ref[i].T[:BACK], sel_ref[i])
+        placed = dot(back_ref[first + pl.program_id(0) * GROUP + h].T[:BACK], sel_ref[i])
         tail = placed[3 * HEAD : 3 * HEAD + 8]
         joint = tail[0:1] + tail[1:2] + tail[2:3]
         far_inner = tail[3:4] + tail[4:5] + tail[5:6]
@@ -258,8 +268,8 @@
         dv_ref[...] = tv_ref[...].T
 
 
-def params():
-    return pltpu.CompilerParams(vmem_limit_bytes=VMEM_LIMIT)
+def params(limit=VMEM_LIMIT):
+    return pltpu.CompilerParams(vmem_limit_bytes=limit)
 
 
 def cost(flops, moved, exps=0):
@@ -278,7 +288,12 @@
             num_scalar_prefetch=1,
             grid=(HEADS // GROUP,),
             in_specs=[nat, nat, nat, pl.BlockSpec((ROWS, WIDTH), lambda i, o: (0, 0)), pl.BlockSpec((COLS, WIDTH), lambda i, o: (i, 0))],
-            out_specs=[per_head(STACK, ROWS), per_head(PICKED, ROWS), per_head(PICKED, PACK)],
+            out_specs=[
+                per_head(STACK, ROWS),
+                per_head(PICKED, ROWS),
+                per_head(PICKED, PACK),
+                pl.BlockSpec((1, GROUP, 128), lambda i, o: (i, 0, 0)),
+            ],
             scratch_shapes=[
                 pltpu.VMEM((GROUP, PICKED, STACK), BF),
                 pltpu.VMEM((GROUP * PICKED, ROWS), F32),
@@ -289,6 +304,7 @@
             jax.ShapeDtypeStruct((HEADS, STACK, ROWS), BF),
             jax.ShapeDtypeStruct((HEADS, PICKED, ROWS), BF),
             jax.ShapeDtypeStruct((HEADS, PICKED, PACK), BF),
+            jax.ShapeDtypeStruct((HEADS // GROUP, GROUP, 128), F32),
         ],
         compiler_params=params(),
         cost_estimate=cost(4 * HEAD_FLOPS, 14 << 20, 1 << 20),
@@ -296,12 +312,13 @@
     )(offsets, q, k, v, g, w)
 
 
-def forward(stack, first, count, before=None):
+def forward(stack, bounds, first, count, before=None):
     carried = [] if before is None else [before]
     return pl.pallas_call(
-        forward_kernel,
+        functools.partial(forward_kernel, first),
         grid=(count // PAIR,),
         in_specs=[pl.BlockSpec((PAIR, STACK, ROWS), lambda i: (i + first // PAIR, 0, 0))]
+        + [pl.BlockSpec(memory_space=pltpu.SMEM)]
         + [pl.BlockSpec(memory_space=pl.ANY)] * len(carried),
         out_specs=[
             pl.BlockSpec((PAIR, ROWS, ROWS), lambda i: (i, 0, 0)),
@@ -314,19 +331,20 @@
             jax.ShapeDtypeStruct((count, 8, ROWS), F32),
         ],
         scratch_shapes=[pltpu.VMEM((PAIR, 8, ROWS), F32)],
-        input_output_aliases={1: 1} if carried else {},
+        input_output_aliases={2: 1} if carried else {},
         compiler_params=params(),
         cost_estimate=cost(2 * count * HEAD_FLOPS, count * (2 << 20), count << 20),
         name="near_forward",
-    )(stack, *carried)
+    )(stack, bounds, *carried)
 
 
 def far(packed):
     return pl.pallas_call(
         far_kernel,
+        in_specs=[pl.BlockSpec(memory_space=pltpu.VMEM)],
         out_shape=jax.ShapeDtypeStruct((ROWS, PACK), BF),
         scratch_shapes=[pltpu.VMEM((ROWS, ROWS), BF), pltpu.VMEM((ROWS, ROWS), BF), pltpu.VMEM((1, 8, ROWS), F32)],
-        compiler_params=params(),
+        compiler_params=params(40 << 20),
         cost_estimate=cost(6 * HEAD_FLOPS, 1 << 20, 1 << 20),
         name="far",
     )(packed)
@@ -342,15 +360,15 @@
             in_specs=[
                 pl.BlockSpec((COLS, ROWS), lambda i, o: (i, 0)),
                 pl.BlockSpec((GROUP, PICKED, ROWS), lambda i, o: (i, 0, 0)),
-                pl.BlockSpec((GROUP, PICKED, PACK), lambda i, o: (i, 0, 0)),
-                pl.BlockSpec((COLS, WIDTH), lambda i, o: (i, 0)),
+                pl.BlockSpec(memory_space=pltpu.VMEM),
+                pl.BlockSpec((WIDTH, WIDTH), lambda i, o: (0, 0)),
                 pl.BlockSpec((ROWS, WIDTH), lambda i, o: (0, 0)),
             ],
             out_specs=[
                 pl.BlockSpec((ROWS, WIDTH), lambda i, o: (0, 0)),
                 pl.BlockSpec((1, devices // groups, SLOT, WIDTH), lambda i, o: (i, 0, 0, 0)),
             ],
-            scratch_shapes=[pltpu.VMEM((COLS, ROWS), BF), pltpu.VMEM((ROWS, WIDTH), F32)],
+            scratch_shapes=[pltpu.VMEM((COLS, ROWS), BF), pltpu.VMEM((ROWS, WIDTH), BF)],
         ),
         out_shape=[
             jax.ShapeDtypeStruct((ROWS, WIDTH), BF),
@@ -378,7 +396,7 @@
                 whole(PICKED, ROWS),
                 pl.BlockSpec((PAIR * HEAD, ROWS), lambda g, h, o: (start + g * steps + h, 0)),
                 piece(8, ROWS),
-                whole(PICKED, PACK),
+                pl.BlockSpec(memory_space=pltpu.VMEM),
             ]
             + [pl.BlockSpec(memory_space=pl.ANY)] * len(before),
             out_specs=[out] * 3,
@@ -394,13 +412,13 @@
 
 def body(queries, keys, values, offsets, w_out, grad_out):
     upstream = grad_out[0]
-    stack, sel, packed = prologue(offsets, queries[0], keys[0], values[0], upstream, w_out)
+    stack, sel, packed, bounds = prologue(offsets, queries[0], keys[0], values[0], upstream, w_out)
     arrived = lax.all_to_all(packed, "ctx", 0, 0, tiled=True)
     half = HEADS // 2
-    e0, att, stat0 = forward(stack, 0, half)
+    e0, att, stat0 = forward(stack, bounds, 0, half)
     far_out = far(arrived.reshape(ROWS, PACK)).reshape(HEADS, PICKED, PACK)
     back = lax.all_to_all(far_out, "ctx", 0, 0, tiled=True)
-    e1, att, stat1 = forward(stack, half, half, att)
+    e1, att, stat1 = forward(stack, bounds, half, half, att)
     devices = lax.axis_size("dp") * lax.axis_size("ctx")
     output, weight_part = project(offsets, att, sel, back, w_out, upstream, devices)
     pieces = lax.all_to_all(weight_part.reshape(devices, SLOT, WIDTH), ("dp", "ctx"), 0, 0, tiled=True)

time: 153 us -> 144 us (0.941)
  Pallas kernels: 109 us -> 100 us
    pallas_call x1, Pallas kernels: 15.1 us -> 10.1 us  [prologue(): pl.pallas_call(prologue_kernel, grid_spec=pltpu.PrefetchScalarGridSpec(nu...]
    pallas_call x3, Pallas kernels: 39.4 us -> 36.5 us  [the longest x2 32.2 us: forward(): pl.pallas_call(functools.partial(forward_kernel, first), grid=(count // P...]
  transfers between devices with their start and end apart: 4 -> 4, of which waited for: 2 -> 2; matrix products, arithmetic and copies ran while one was open for 0% -> 0% of each run, Pallas kernels for 52% -> 54%
where the time goes in v3:
time: 144 us; the launch traced here: 143 us
  Pallas kernels  100 us (69%)
  starting transfers between devices  34.1 us (24%)
  waiting for transfers between devices  4.6 us (3%)
  local copies, waits for them, and re-layouts  2.12 us (1%)
  other arithmetic  1.89 us (1%)
    pallas_call x2, Pallas kernels, backward(): pl.pallas_call(functools.partial(backward_kernel, first), grid_spec=pltpu...  44.9 us
    pallas_call x2, Pallas kernels, forward(): pl.pallas_call(functools.partial(forward_kernel, first), grid=(count // P...  32.2 us
    pallas_call x1, Pallas kernels, prologue(): pl.pallas_call(prologue_kernel, grid_spec=pltpu.PrefetchScalarGridSpec(nu...  10.1 us
    all_to_all x1, starting transfers between devices, body(): lax.all_to_all(weight_part.reshape(devices, SLOT, WIDTH), ('dp', 'ctx'),...  9.43 us
    all_to_all x1, starting transfers between devices, body(): arrived = lax.all_to_all(packed, 'ctx', 0, 0, tiled=True)  9.29 us
    pallas_call x1, Pallas kernels, project(): pl.pallas_call(output_kernel, grid_spec=pltpu.PrefetchScalarGridSpec(num_...  8.45 us
    all_to_all x1, starting transfers between devices, body(): back = lax.all_to_all(far_out, 'ctx', 0, 0, tiled=True)  7.97 us
    all_to_all x1, starting transfers between devices, body(): lax.all_to_all(jnp.broadcast_to(total[None], pieces.shape), ('dp', 'ctx')...  7.45 us
  transfers between devices with their start and end apart: 4, of which 2 were waited for; matrix products, arithmetic and copies ran while one was open for 0% of the time, Pallas kernels for 54%

profile of v3, /device:TPU:1, one launch (start us, length us, event | category | flops | bytes accessed | tf_op | source)
XLA Modules:
  0.0 143.4 jit_solution(8824828461229377650)
XLA Ops:
  0.6 10.1 %prologue.1 = (bf16[16,192,1024]{2,1,0:T(8,128)(2,1)}, bf16[16,64,1024]{2,1,0:T(8,128)(2,1)}, bf16[16,64,256]{2,1,0:T(8,128)(2,1)}, f32[2,8,128]{2,1,0:T(8,128)}) custom-call(s32[16]{0:T(128)} %off_ref.7, bf16[1024,768]{1,0:T(8,128)(2,1)} %bitcast.17, bf16[1024,768]{1,0:T(8,128)(2,1)} %bitcast.18, bf16[1024,768]{1,0:T(8,128)(2,1)} %bitcast.19, ...), custom_call_target="tpu_custom_call" | custom-call | flops 2147483648 | bytes 14680064 | tf_op jit(solution)/shard_map/prologue/pallas_call | solution.py:285
  10.7 9.3 %all-to-all-start = ((bf16[16,64,256]{2,1,0:T(8,128)(2,1)}), bf16[16,64,256]{2,1,0:T(8,128)(2,1)S(1)}, u32[]{:S(2)}, u32[]{:S(2)}) async-start(bf16[16,64,256]{2,1,0:T(8,128)(2,1)} %get-tuple-element.28), calls=%async_computation | async-start | bytes 1048576 | tf_op jit(solution)/shard_map/all_to_all | solution.py:416
  20.0 16.1 %near_forward.2 = (bf16[8,1024,1024]{2,1,0:T(8,128)(2,1)}, bf16[768,1024]{1,0:T(8,128)(2,1)}, f32[8,8,1024]{2,1,0:T(8,128)}) custom-call(bf16[16,192,1024]{2,1,0:T(8,128)(2,1)} %get-tuple-element.23.stack_ref, f32[2,8,128]{2,1,0:T(8,128)} %get-tuple-element.24.bound_ref), custom_call_target="tpu_custom_call" | custom-call | flops 8589934592 | bytes 16777216 | tf_op jit(solution)/shard_map/near_forward/pallas_call | solution.py:317
  36.1 0.0 all-to-all-done
  36.1 4.3 %far.1 = bf16[1024,256]{1,0:T(8,128)(2,1)} custom-call(bf16[1024,256]{1,0:T(8,128)(2,1)S(1)} %bitcast.13), custom_call_target="tpu_custom_call" | custom-call | flops 3221225472 | bytes 1048576 | tf_op jit(solution)/shard_map/far/pallas_call | solution.py:342
  40.4 8.0 %all-to-all-start.1 = ((bf16[16,64,256]{2,1,0:T(8,128)(2,1)}), bf16[16,64,256]{2,1,0:T(8,128)(2,1)S(1)}, u32[]{:S(2)}, u32[]{:S(2)}) async-start(bf16[16,64,256]{2,1,0:T(8,128)(2,1)} %bitcast.5), calls=%async_computation.1 | async-start | bytes 1048576 | tf_op jit(solution)/shard_map/all_to_all | solution.py:420
  48.4 16.1 %near_forward.3 = (bf16[8,1024,1024]{2,1,0:T(8,128)(2,1)}, bf16[768,1024]{1,0:T(8,128)(2,1)}, f32[8,8,1024]{2,1,0:T(8,128)}) custom-call(bf16[16,192,1024]{2,1,0:T(8,128)(2,1)} %get-tuple-element.23.stack_ref, f32[2,8,128]{2,1,0:T(8,128)} %get-tuple-element.24.bound_ref, bf16[768,1024]{1,0:T(8,128)(2,1)} %get-tuple-element.25.refs_0_), custom_call_target="tpu_custom_call", output_to_operand_aliasing={{1}: (2, {})} | custom-call | flops 8589934592 | bytes 16777216 | tf_op jit(solution)/shard_map/near_forward/pallas_call | solution.py:317
  64.5 0.0 all-to-all-done.1.back_ref
  64.5 0.0 copy-start
  64.5 0.8 copy-done
  65.3 8.4 %project.1 = (bf16[1024,768]{1,0:T(8,128)(2,1)}, bf16[2,64,8,768]{3,2,1,0:T(8,128)(2,1)}) custom-call(s32[16]{0:T(128)} %off_ref.7, bf16[768,1024]{1,0:T(8,128)(2,1)} %get-tuple-element.26.att_ref, bf16[16,64,1024]{2,1,0:T(8,128)(2,1)} %get-tuple-element.27.sel_ref, bf16[16,64,256]{2,1,0:T(8,128)(2,1)} %copy-done, bf16[768,768]{1,0:T(8,128)(2,1)} %w_ref.3, ...), custom_call_target="tpu_custom_call" | custom-call | flops 2415919104 | bytes 10485760 | tf_op jit(solution)/shard_map/project/pallas_call | solution.py:355
  73.8 9.4 %all-to-all-start.2 = ((bf16[128,8,768]{2,1,0:T(8,128)(2,1)}), bf16[128,8,768]{2,1,0:T(8,128)(2,1)S(1)}, u32[]{:S(2)}, u32[]{:S(2)}) async-start(bf16[128,8,768]{2,1,0:T(8,128)(2,1)} %bitcast.16), calls=%async_computation.2 | async-start | bytes 3145728 | tf_op jit(solution)/shard_map/all_to_all | solution.py:424
  83.2 22.4 %near_backward.2 = (bf16[1024,768]{1,0:T(8,128)(2,1)}, bf16[1024,768]{1,0:T(8,128)(2,1)}, bf16[1024,768]{1,0:T(8,128)(2,1)}) custom-call(s32[16]{0:T(128)} %off_ref.7, bf16[8,1024,1024]{2,1,0:T(8,128)(2,1)} %get-tuple-element.32.e_ref, bf16[16,192,1024]{2,1,0:T(8,128)(2,1)} %get-tuple-element.23.stack_ref, bf16[16,64,1024]{2,1,0:T(8,128)(2,1)} %get-tuple-element.27.sel_ref, ...), custom_call_target="tpu_custom_call" | custom-call | flops 17179869184 | bytes 16777216 | tf_op jit(solution)/shard_map/near_backward/pallas_call | solution.py:388
  105.7 2.3 %all-to-all-done.2 = bf16[128,8,768]{2,1,0:T(8,128)(2,1)S(1)} async-done(((bf16[128,8,768]{2,1,0:T(8,128)(2,1)}), bf16[128,8,768]{2,1,0:T(8,128)(2,1)S(1)}, u32[]{:S(2)}, u32[]{:S(2)}) %all-to-all-start.2) | async-done | bytes 1572896 | tf_op jit(solution)/shard_map/all_to_all | solution.py:424
  108.0 0.3 reduce_sum.12
  108.3 1.3 broadcast_in_dim.22
  109.5 7.5 %all-to-all-start.3 = ((bf16[128,8,768]{2,1,0:T(8,128)(2,1)}), bf16[128,8,768]{2,1,0:T(8,128)(2,1)S(1)}, u32[]{:S(2)}, u32[]{:S(2)}) async-start(bf16[128,8,768]{2,1,0:T(8,128)(2,1)} %broadcast_in_dim.22), calls=%async_computation.3 | async-start | bytes 3145728 | tf_op jit(solution)/shard_map/all_to_all | solution.py:427
  117.0 22.5 %near_backward.3 = (bf16[1024,768]{1,0:T(8,128)(2,1)}, bf16[1024,768]{1,0:T(8,128)(2,1)}, bf16[1024,768]{1,0:T(8,128)(2,1)}) custom-call(s32[16]{0:T(128)} %off_ref.7, bf16[8,1024,1024]{2,1,0:T(8,128)(2,1)} %get-tuple-element.30.e_ref, ...), custom_call_target="tpu_custom_call", output_to_operand_aliasing={{0}: (7, {}), {1}: (8, {}), {2}: (9, {})} | custom-call | flops 17179869184 | bytes 16777216 | tf_op jit(solution)/shard_map/near_backward/pallas_call | solution.py:388
  139.5 2.3 %all-to-all-done.3 = bf16[128,8,768]{2,1,0:T(8,128)(2,1)S(1)} async-done(((bf16[128,8,768]{2,1,0:T(8,128)(2,1)}), bf16[128,8,768]{2,1,0:T(8,128)(2,1)S(1)}, u32[]{:S(2)}, u32[]{:S(2)}) %all-to-all-start.3) | async-done | bytes 1572896 | tf_op jit(solution)/shard_map/all_to_all | solution.py:427
  141.8 1.6 %convert_multiply_fusion = f32[2,48,8,768]{3,2,1,0:T(8,128)} fusion(bf16[2,64,8,768]{3,2,1,0:T(8,128)(2,1)S(1)} %bitcast.14), kind=kLoop, calls=%fused_computation | loop fusion | flops 1179648 | bytes 3538944 | tf_op jit(solution)/shard_map/mul | solution.py:431
Async XLA Ops:
  10.7 25.4 %all-to-all-start = ((bf16[16,64,256]{2,1,0:T(8,128)(2,1)}), bf16[16,64,256]{2,1,0:T(8,128)(2,1)S(1)}, u32[]{:S(2)}, u32[]{:S(2)}) async-start(bf16[16,64,256]{2,1,0:T(8,128)(2,1)} %get-tuple-element.28), calls=%async_computation | async-start | bytes 1048576 | tf_op jit(solution)/shard_map/all_to_all | solution.py:416
  40.4 24.1 %all-to-all-start.1 = ((bf16[16,64,256]{2,1,0:T(8,128)(2,1)}), bf16[16,64,256]{2,1,0:T(8,128)(2,1)S(1)}, u32[]{:S(2)}, u32[]{:S(2)}) async-start(bf16[16,64,256]{2,1,0:T(8,128)(2,1)} %bitcast.5), calls=%async_computation.1 | async-start | bytes 1048576 | tf_op jit(solution)/shard_map/all_to_all | solution.py:420
  64.5 0.8 copy-start
  73.8 34.2 %all-to-all-start.2 = ((bf16[128,8,768]{2,1,0:T(8,128)(2,1)}), bf16[128,8,768]{2,1,0:T(8,128)(2,1)S(1)}, u32[]{:S(2)}, u32[]{:S(2)}) async-start(bf16[128,8,768]{2,1,0:T(8,128)(2,1)} %bitcast.16), calls=%async_computation.2 | async-start | bytes 3145728 | tf_op jit(solution)/shard_map/all_to_all | solution.py:424
  109.5 32.2 %all-to-all-start.3 = ((bf16[128,8,768]{2,1,0:T(8,128)(2,1)}), bf16[128,8,768]{2,1,0:T(8,128)(2,1)S(1)}, u32[]{:S(2)}, u32[]{:S(2)}) async-start(bf16[128,8,768]{2,1,0:T(8,128)(2,1)} %broadcast_in_dim.22), calls=%async_computation.3 | async-start | bytes 3145728 | tf_op jit(solution)/shard_map/all_to_all | solution.py:427

commit v4 on v3

--- a/solution.py
+++ b/solution.py
@@ -97,22 +97,15 @@
 
 
 def gradient_operands(value, dattend, ratio, inner):
-    hi, lo = split2(dattend * ratio)
-    ihi, ilo = split2(-inner * ratio)
-    tail = rows16([ihi.astype(F32), ilo.astype(F32)]).astype(BF)
-    pad = jnp.zeros((16, ROWS), BF)
-    right = jnp.concatenate([hi, lo, tail, pad], axis=0)
-    one = jnp.ones((1, ROWS), F32)
-    left = jnp.concatenate([value, value, rows16([one, one]).astype(BF), pad], axis=0).T
-    return left, right, hi
+    return value.T, dattend.astype(BF), (dattend * ratio).astype(BF), ratio, inner
 
 
 def gradient_chunks(e_ref, query, key, operands, ds_ref):
-    left, right, hi = operands
+    left, right, hi, ratio, inner = operands
     starts = range(0, ROWS, STEP)
     def first(start):
         rows = slice(start, start + STEP)
-        ds_ref[rows, :] = dot(left[rows, :], right).astype(BF) * e_ref[rows, :]
+        ds_ref[rows, :] = ((dot(left[rows, :], right) - inner) * ratio).astype(BF) * e_ref[rows, :]
     dq, dks, dvs = None, [], []
     query_rows = query.T
     first(0)
@@ -332,7 +325,7 @@
         ],
         scratch_shapes=[pltpu.VMEM((PAIR, 8, ROWS), F32)],
         input_output_aliases={2: 1} if carried else {},
-        compiler_params=params(),
+        compiler_params=params(48 << 20 if carried else VMEM_LIMIT),
         cost_estimate=cost(2 * count * HEAD_FLOPS, count * (2 << 20), count << 20),
         name="near_forward",
     )(stack, bounds, *carried)
@@ -374,7 +367,7 @@
             jax.ShapeDtypeStruct((ROWS, WIDTH), BF),
             jax.ShapeDtypeStruct((groups, devices // groups, SLOT, WIDTH), BF),
         ],
-        compiler_params=params(),
+        compiler_params=params(48 << 20),
         cost_estimate=cost(4 * ROWS * WIDTH * WIDTH, 10 << 20),
         name="project",
     )(offsets, att, sel, back, w, g)

time: 144 us -> 142 us (0.986)
  Pallas kernels: 100 us -> 98.2 us
where the time goes in v4:
time: 142 us
  Pallas kernels  98.2 us (69%)
  starting transfers between devices  33.5 us (24%)
  waiting for transfers between devices  5.47 us (4%)
  local copies, waits for them, and re-layouts  2.02 us (1%)
  other arithmetic  1.89 us (1%)
    pallas_call x2, Pallas kernels, backward(): pl.pallas_call(functools.partial(backward_kernel, first), grid_spec=pltpu...  44.1 us
    pallas_call x2, Pallas kernels, forward(): pl.pallas_call(functools.partial(forward_kernel, first), grid=(count // P...  32.2 us
    pallas_call x1, Pallas kernels, prologue(): pl.pallas_call(prologue_kernel, grid_spec=pltpu.PrefetchScalarGridSpec(nu...  10.1 us
    all_to_all x1, starting transfers between devices, body(): lax.all_to_all(weight_part.reshape(devices, SLOT, WIDTH), ('dp', 'ctx'),...  9.44 us
    all_to_all x1, starting transfers between devices, body(): arrived = lax.all_to_all(packed, 'ctx', 0, 0, tiled=True)  9.29 us
    all_to_all x1, starting transfers between devices, body(): back = lax.all_to_all(far_out, 'ctx', 0, 0, tiled=True)  7.73 us
    pallas_call x1, Pallas kernels, project(): pl.pallas_call(output_kernel, grid_spec=pltpu.PrefetchScalarGridSpec(num_...  7.7 us
    all_to_all x1, starting transfers between devices, body(): lax.all_to_all(jnp.broadcast_to(total[None], pieces.shape), ('dp', 'ctx')...  7.02 us
  transfers between devices with their start and end apart: 4, of which 2 were waited for; matrix products, arithmetic and copies ran while one was open for 0% of the time, Pallas kernels for 54%

profile of v4, /device:TPU:1, one launch (start us, length us, event | category | flops | bytes accessed | tf_op | source)
XLA Modules:
  0.0 141.7 jit_solution(10779500797715824332)
XLA Ops:
  0.6 10.1 %prologue.1 = (bf16[16,192,1024]{2,1,0:T(8,128)(2,1)}, bf16[16,64,1024]{2,1,0:T(8,128)(2,1)}, bf16[16,64,256]{2,1,0:T(8,128)(2,1)}, f32[2,8,128]{2,1,0:T(8,128)}) custom-call(s32[16]{0:T(128)} %off_ref.7, bf16[1024,768]{1,0:T(8,128)(2,1)} %bitcast.16, bf16[1024,768]{1,0:T(8,128)(2,1)} %bitcast.17, bf16[1024,768]{1,0:T(8,128)(2,1)} %bitcast.18, ...), custom_call_target="tpu_custom_call" | custom-call | flops 2147483648 | bytes 14680064 | tf_op jit(solution)/shard_map/prologue/pallas_call | solution.py:278
  10.7 9.3 %all-to-all-start = ((bf16[16,64,256]{2,1,0:T(8,128)(2,1)}), bf16[16,64,256]{2,1,0:T(8,128)(2,1)S(1)}, u32[]{:S(2)}, u32[]{:S(2)}) async-start(bf16[16,64,256]{2,1,0:T(8,128)(2,1)} %get-tuple-element.28), calls=%async_computation | async-start | bytes 1048576 | tf_op jit(solution)/shard_map/all_to_all | solution.py:409
  20.0 16.1 %near_forward.2 = (bf16[8,1024,1024]{2,1,0:T(8,128)(2,1)}, bf16[768,1024]{1,0:T(8,128)(2,1)}, f32[8,8,1024]{2,1,0:T(8,128)}) custom-call(bf16[16,192,1024]{2,1,0:T(8,128)(2,1)} %get-tuple-element.23.stack_ref, f32[2,8,128]{2,1,0:T(8,128)} %get-tuple-element.24.bound_ref), custom_call_target="tpu_custom_call" | custom-call | flops 8589934592 | bytes 16777216 | tf_op jit(solution)/shard_map/near_forward/pallas_call | solution.py:310
  36.1 0.0 all-to-all-done
  36.1 0.0 copy-start.3
  36.1 0.0 copy-start.5
  36.1 4.2 %far.1 = bf16[1024,256]{1,0:T(8,128)(2,1)} custom-call(bf16[1024,256]{1,0:T(8,128)(2,1)S(1)} %bitcast.13), custom_call_target="tpu_custom_call" | custom-call | flops 3221225472 | bytes 1048576 | tf_op jit(solution)/shard_map/far/pallas_call | solution.py:335
  40.3 7.7 %all-to-all-start.1 = ((bf16[16,64,256]{2,1,0:T(8,128)(2,1)}), bf16[16,64,256]{2,1,0:T(8,128)(2,1)S(1)}, u32[]{:S(2)}, u32[]{:S(2)}) async-start(bf16[16,64,256]{2,1,0:T(8,128)(2,1)} %bitcast.5), calls=%async_computation.1 | async-start | bytes 1048576 | tf_op jit(solution)/shard_map/all_to_all | solution.py:413
  48.0 0.0 copy-done.3
  48.0 0.0 copy-done.5
  48.0 0.0 copy-start.1
  48.0 0.0 copy-start.2
  48.1 16.1 %near_forward.3 = (bf16[8,1024,1024]{2,1,0:T(8,128)(2,1)}, bf16[768,1024]{1,0:T(8,128)(2,1)S(1)}, f32[8,8,1024]{2,1,0:T(8,128)S(1)}) custom-call(bf16[16,192,1024]{2,1,0:T(8,128)(2,1)} %get-tuple-element.23.stack_ref, f32[2,8,128]{2,1,0:T(8,128)S(1)} %copy-done.5, bf16[768,1024]{1,0:T(8,128)(2,1)S(1)} %copy-done.3), custom_call_target="tpu_custom_call", output_to_operand_aliasing={{1}: (2, {})} | custom-call | flops 8589934592 | bytes 16777216 | tf_op jit(solution)/shard_map/near_forward/pallas_call | solution.py:310
  64.1 0.0 copy-start.6
  64.1 0.7 copy-done.6
  64.8 0.0 copy-start.4
  64.8 0.0 all-to-all-done.1.back_ref
  64.8 0.0 copy-start
  64.8 0.0 copy-done.1
  64.8 0.0 copy-done.2
  64.9 7.7 %project.1 = (bf16[1024,768]{1,0:T(8,128)(2,1)}, bf16[2,64,8,768]{3,2,1,0:T(8,128)(2,1)}) custom-call(s32[16]{0:T(128)S(1)} %copy-done.2, bf16[768,1024]{1,0:T(8,128)(2,1)S(1)} %get-tuple-element.26.att_ref, bf16[16,64,1024]{2,1,0:T(8,128)(2,1)} %get-tuple-element.27.sel_ref, bf16[16,64,256]{2,1,0:T(8,128)(2,1)S(1)} %all-to-all-done.1.back_ref, ...), custom_call_target="tpu_custom_call" | custom-call | flops 2415919104 | bytes 10485760 | tf_op jit(solution)/shard_map/project/pallas_call | solution.py:348
  72.6 0.0 copy-done.4
  72.6 0.0 copy-done
  72.6 9.4 %all-to-all-start.2 = ((bf16[128,8,768]{2,1,0:T(8,128)(2,1)}), bf16[128,8,768]{2,1,0:T(8,128)(2,1)S(1)}, u32[]{:S(2)}, u32[]{:S(2)}) async-start(bf16[128,8,768]{2,1,0:T(8,128)(2,1)} %bitcast.10), calls=%async_computation.2 | async-start | bytes 3145728 | tf_op jit(solution)/shard_map/all_to_all | solution.py:417
  82.0 22.0 %near_backward.2 = (bf16[1024,768]{1,0:T(8,128)(2,1)}, bf16[1024,768]{1,0:T(8,128)(2,1)}, bf16[1024,768]{1,0:T(8,128)(2,1)}) custom-call(s32[16]{0:T(128)} %off_ref.7, bf16[8,1024,1024]{2,1,0:T(8,128)(2,1)} %get-tuple-element.32.e_ref, bf16[16,192,1024]{2,1,0:T(8,128)(2,1)} %get-tuple-element.23.stack_ref, bf16[16,64,1024]{2,1,0:T(8,128)(2,1)} %get-tuple-element.27.sel_ref, ...), custom_call_target="tpu_custom_call" | custom-call | flops 17179869184 | bytes 16777216 | tf_op jit(solution)/shard_map/near_backward/pallas_call | solution.py:381
  104.0 2.8 %all-to-all-done.2 = bf16[128,8,768]{2,1,0:T(8,128)(2,1)S(1)} async-done(((bf16[128,8,768]{2,1,0:T(8,128)(2,1)}), bf16[128,8,768]{2,1,0:T(8,128)(2,1)S(1)}, u32[]{:S(2)}, u32[]{:S(2)}) %all-to-all-start.2) | async-done | bytes 1572896 | tf_op jit(solution)/shard_map/all_to_all | solution.py:417
  106.8 0.3 reduce_sum.12
  107.1 1.3 broadcast_in_dim.22
  108.3 7.0 %all-to-all-start.3 = ((bf16[128,8,768]{2,1,0:T(8,128)(2,1)}), bf16[128,8,768]{2,1,0:T(8,128)(2,1)S(1)}, u32[]{:S(2)}, u32[]{:S(2)}) async-start(bf16[128,8,768]{2,1,0:T(8,128)(2,1)} %broadcast_in_dim.22), calls=%async_computation.3 | async-start | bytes 3145728 | tf_op jit(solution)/shard_map/all_to_all | solution.py:420
  115.4 22.0 %near_backward.3 = (bf16[1024,768]{1,0:T(8,128)(2,1)}, bf16[1024,768]{1,0:T(8,128)(2,1)}, bf16[1024,768]{1,0:T(8,128)(2,1)}) custom-call(s32[16]{0:T(128)} %off_ref.7, bf16[8,1024,1024]{2,1,0:T(8,128)(2,1)} %get-tuple-element.30.e_ref, ...), custom_call_target="tpu_custom_call", output_to_operand_aliasing={{0}: (7, {}), {1}: (8, {}), {2}: (9, {})} | custom-call | flops 17179869184 | bytes 16777216 | tf_op jit(solution)/shard_map/near_backward/pallas_call | solution.py:381
  137.4 2.7 %all-to-all-done.3 = bf16[128,8,768]{2,1,0:T(8,128)(2,1)S(1)} async-done(((bf16[128,8,768]{2,1,0:T(8,128)(2,1)}), bf16[128,8,768]{2,1,0:T(8,128)(2,1)S(1)}, u32[]{:S(2)}, u32[]{:S(2)}) %all-to-all-start.3) | async-done | bytes 1572896 | tf_op jit(solution)/shard_map/all_to_all | solution.py:420
  140.1 1.6 %convert_multiply_fusion = f32[2,48,8,768]{3,2,1,0:T(8,128)} fusion(bf16[2,64,8,768]{3,2,1,0:T(8,128)(2,1)S(1)} %bitcast.14), kind=kLoop, calls=%fused_computation | loop fusion | flops 1179648 | bytes 3538944 | tf_op jit(solution)/shard_map/mul | solution.py:424
Async XLA Ops:
  10.7 25.4 %all-to-all-start = ((bf16[16,64,256]{2,1,0:T(8,128)(2,1)}), bf16[16,64,256]{2,1,0:T(8,128)(2,1)S(1)}, u32[]{:S(2)}, u32[]{:S(2)}) async-start(bf16[16,64,256]{2,1,0:T(8,128)(2,1)} %get-tuple-element.28), calls=%async_computation | async-start | bytes 1048576 | tf_op jit(solution)/shard_map/all_to_all | solution.py:409
  36.1 11.9 %copy-start.3 = (bf16[768,1024]{1,0:T(8,128)(2,1)S(1)}, bf16[768,1024]{1,0:T(8,128)(2,1)}, u32[]{:S(2)}) copy-start(bf16[768,1024]{1,0:T(8,128)(2,1)} %get-tuple-element.25.refs_0_) | copy-start | bytes 4718596
  36.1 11.9 %copy-start.5 = (f32[2,8,128]{2,1,0:T(8,128)S(1)}, f32[2,8,128]{2,1,0:T(8,128)}, u32[]{:S(2)}) copy-start(f32[2,8,128]{2,1,0:T(8,128)} %get-tuple-element.24.bound_ref) | copy-start | bytes 24580
  40.3 24.6 %all-to-all-start.1 = ((bf16[16,64,256]{2,1,0:T(8,128)(2,1)}), bf16[16,64,256]{2,1,0:T(8,128)(2,1)S(1)}, u32[]{:S(2)}, u32[]{:S(2)}) async-start(bf16[16,64,256]{2,1,0:T(8,128)(2,1)} %bitcast.5), calls=%async_computation.1 | async-start | bytes 1048576 | tf_op jit(solution)/shard_map/all_to_all | solution.py:413
  48.0 16.8 %copy-start.1 = (bf16[768,768]{1,0:T(8,128)(2,1)S(1)}, bf16[768,768]{1,0:T(8,128)(2,1)}, u32[]{:S(2)}) copy-start(bf16[768,768]{1,0:T(8,128)(2,1)} %w_ref.3) | copy-start | bytes 3538948
  48.0 16.8 %copy-start.2 = (s32[16]{0:T(128)S(1)}, s32[16]{0:T(128)}, u32[]{:S(2)}) copy-start(s32[16]{0:T(128)} %off_ref.7) | copy-start | bytes 196
  64.1 0.7 copy-start.6
  64.8 7.7 %copy-start.4 = (bf16[768,1024]{1,0:T(8,128)(2,1)}, bf16[768,1024]{1,0:T(8,128)(2,1)S(1)}, u32[]{:S(2)}) copy-start(bf16[768,1024]{1,0:T(8,128)(2,1)S(1)} %get-tuple-element.26.att_ref) | copy-start | bytes 4718596
  64.8 7.7 %copy-start = (bf16[16,64,256]{2,1,0:T(8,128)(2,1)}, bf16[16,64,256]{2,1,0:T(8,128)(2,1)S(1)}, u32[]{:S(2)}) copy-start(bf16[16,64,256]{2,1,0:T(8,128)(2,1)S(1)} %all-to-all-done.1.back_ref) | copy-start | bytes 1572868
  72.6 34.2 %all-to-all-start.2 = ((bf16[128,8,768]{2,1,0:T(8,128)(2,1)}), bf16[128,8,768]{2,1,0:T(8,128)(2,1)S(1)}, u32[]{:S(2)}, u32[]{:S(2)}) async-start(bf16[128,8,768]{2,1,0:T(8,128)(2,1)} %bitcast.10), calls=%async_computation.2 | async-start | bytes 3145728 | tf_op jit(solution)/shard_map/all_to_all | solution.py:417
  108.3 31.8 %all-to-all-start.3 = ((bf16[128,8,768]{2,1,0:T(8,128)(2,1)}), bf16[128,8,768]{2,1,0:T(8,128)(2,1)S(1)}, u32[]{:S(2)}, u32[]{:S(2)}) async-start(bf16[128,8,768]{2,1,0:T(8,128)(2,1)} %broadcast_in_dim.22), calls=%async_computation.3 | async-start | bytes 3145728 | tf_op jit(solution)/shard_map/all_to_all | solution.py:420

commit v5 on v4

--- a/solution.py
+++ b/solution.py
@@ -23,6 +23,8 @@
 PAIR = 2
 SAFE = 64.0
 SLOT = 8
+LANES = 128
+MAIN = WIDTH - LANES
 ROOT = HEAD**-0.5
 SCALE = ROOT * 1.4426950408889634
 BF = jnp.bfloat16
@@ -216,8 +218,13 @@
         placed = dot(back_ref[group * GROUP + h].T[BACK : BACK + HEAD], sel_ref[h]).astype(BF)
         full_ref[rows, :] = jnp.where(tile == off_ref[group * GROUP + h], placed, att_ref[rows, :])
     att = full_ref[...]
-    wg_ref[0, : COLS // SLOT] = dot(att, g_ref[...]).reshape(COLS // SLOT, SLOT, WIDTH).astype(BF)
-    wg_ref[0, COLS // SLOT :] = jnp.zeros((wg_ref.shape[1] - COLS // SLOT, SLOT, WIDTH), BF)
+    grad = dot(att, g_ref[...]).reshape(COLS // SLOT, SLOT, WIDTH).astype(BF)
+    main, extra = COLS // SLOT, wg_ref.shape[1] - COLS // SLOT
+    wg_ref[0, :main] = grad[:, :, :MAIN]
+    tail = grad[:, :, MAIN:].reshape(extra, main // extra, SLOT, LANES)
+    for i in range(MAIN // LANES):
+        piece = tail[:, i] if i < main // extra else jnp.zeros((extra, SLOT, LANES), BF)
+        wg_ref[0, main:, :, i * LANES : (i + 1) * LANES] = piece
     for g in range(HEADS // GROUP):
 
         @pl.when(group == g)
@@ -259,6 +266,14 @@
         dq_ref[...] = tq_ref[...].T
         dk_ref[...] = tk_ref[...].T
         dv_ref[...] = tv_ref[...].T
+
+
+def unpack_kernel(scale, in_ref, out_ref):
+    main, extra = COLS // SLOT, in_ref.shape[1] - COLS // SLOT
+    out_ref[:, :MAIN] = in_ref[0, :main].astype(F32).reshape(COLS, MAIN) * scale
+    tail = in_ref[0, main:].astype(F32) * scale
+    tail = jnp.stack([tail[:, :, i * LANES : (i + 1) * LANES] for i in range(main // extra)], axis=1)
+    out_ref[:, MAIN:] = tail.reshape(COLS, LANES)
 
 
 def params(limit=VMEM_LIMIT):
@@ -325,7 +340,7 @@
         ],
         scratch_shapes=[pltpu.VMEM((PAIR, 8, ROWS), F32)],
         input_output_aliases={2: 1} if carried else {},
-        compiler_params=params(48 << 20 if carried else VMEM_LIMIT),
+        compiler_params=params(VMEM_LIMIT),
         cost_estimate=cost(2 * count * HEAD_FLOPS, count * (2 << 20), count << 20),
         name="near_forward",
     )(stack, bounds, *carried)
@@ -359,18 +374,32 @@
             ],
             out_specs=[
                 pl.BlockSpec((ROWS, WIDTH), lambda i, o: (0, 0)),
-                pl.BlockSpec((1, devices // groups, SLOT, WIDTH), lambda i, o: (i, 0, 0, 0)),
+                pl.BlockSpec((1, devices // groups, SLOT, MAIN), lambda i, o: (i, 0, 0, 0)),
             ],
             scratch_shapes=[pltpu.VMEM((COLS, ROWS), BF), pltpu.VMEM((ROWS, WIDTH), BF)],
         ),
         out_shape=[
             jax.ShapeDtypeStruct((ROWS, WIDTH), BF),
-            jax.ShapeDtypeStruct((groups, devices // groups, SLOT, WIDTH), BF),
+            jax.ShapeDtypeStruct((groups, devices // groups, SLOT, MAIN), BF),
         ],
         compiler_params=params(48 << 20),
         cost_estimate=cost(4 * ROWS * WIDTH * WIDTH, 10 << 20),
         name="project",
     )(offsets, att, sel, back, w, g)
+
+
+def unpack(packed, devices):
+    groups = HEADS // GROUP
+    return pl.pallas_call(
+        functools.partial(unpack_kernel, (ROWS * devices) ** -0.5),
+        grid=(groups,),
+        in_specs=[pl.BlockSpec((1, devices // groups, SLOT, MAIN), lambda i: (i, 0, 0, 0))],
+        out_specs=pl.BlockSpec((COLS, WIDTH), lambda i: (i, 0)),
+        out_shape=jax.ShapeDtypeStruct((WIDTH, WIDTH), F32),
+        compiler_params=params(40 << 20),
+        cost_estimate=cost(WIDTH * WIDTH, 4 << 20),
+        name="unpack",
+    )(packed.reshape(groups, devices // groups, SLOT, MAIN))
 
 
 def backward(offsets, e, stack, sel, att, stat, back, first, count, before=()):
@@ -414,14 +443,12 @@
     e1, att, stat1 = forward(stack, bounds, half, half, att)
     devices = lax.axis_size("dp") * lax.axis_size("ctx")
     output, weight_part = project(offsets, att, sel, back, w_out, upstream, devices)
-    pieces = lax.all_to_all(weight_part.reshape(devices, SLOT, WIDTH), ("dp", "ctx"), 0, 0, tiled=True)
+    pieces = lax.all_to_all(weight_part.reshape(devices, SLOT, MAIN), ("dp", "ctx"), 0, 0, tiled=True)
     grads = backward(offsets, e0, stack, sel, att, stat0, back, 0, half)
     total = jnp.sum(pieces.astype(F32), axis=0).astype(BF)
     whole = lax.all_to_all(jnp.broadcast_to(total[None], pieces.shape), ("dp", "ctx"), 0, 0, tiled=True)
     dq, dk, dv = backward(offsets, e1, stack, sel, att, stat1, back, half, half, grads)
-    groups = HEADS // GROUP
-    whole = whole.reshape(groups, devices // groups, SLOT, WIDTH)[:, : COLS // SLOT].reshape(WIDTH, WIDTH)
-    weight_grad = whole.astype(F32) * (ROWS * devices) ** -0.5
+    weight_grad = unpack(whole, devices)
     return output[None], dq[None], dk[None], dv[None], weight_grad
 
 

time: 142 us -> 140 us (0.986)
  waiting for transfers between devices: 5.47 us -> 0.02 us
  starting transfers between devices: 33.5 us -> 35.8 us
  Pallas kernels: 98.2 us -> 99.9 us
  other arithmetic: 1.89 us -> 0.24 us
    all_to_all x1, starting transfers between devices: 7.02 us -> 9.79 us  [body(): lax.all_to_all(jnp.broadcast_to(total[None], pieces.shape), ('dp', 'ctx')...]
    all_to_all x1, waiting for transfers between devices: 2.76 us -> 0.02 us  [body(): lax.all_to_all(weight_part.reshape(devices, SLOT, MAIN), ('dp', 'ctx'), 0...]
    all_to_all x1, waiting for transfers between devices: 2.71 us -> 0.01 us  [body(): lax.all_to_all(jnp.broadcast_to(total[None], pieces.shape), ('dp', 'ctx')...]
    mul x1 -> x0, other arithmetic: 1.62 us -> none  [body(): weight_grad = whole.astype(F32) * (ROWS * devices) ** (-0.5)]
    pallas_call x0 -> x1, Pallas kernels: none -> 1.52 us  [unpack(): pl.pallas_call(functools.partial(unpack_kernel, (ROWS * devices) ** (-0.5...]
  transfers between devices with their start and end apart: 4 -> 4, of which waited for: 2 -> 0; matrix products, arithmetic and copies ran while one was open for 0% -> 0% of each run, Pallas kernels for 54% -> 55%
where the time goes in v5:
time: 140 us; the launch traced here: 139 us
  Pallas kernels  99.9 us (71%)
  starting transfers between devices  35.8 us (26%)
  local copies, waits for them, and re-layouts  2.78 us (2%)
    pallas_call x2, Pallas kernels, backward(): pl.pallas_call(functools.partial(backward_kernel, first), grid_spec=pltpu...  44.1 us
    pallas_call x2, Pallas kernels, forward(): pl.pallas_call(functools.partial(forward_kernel, first), grid=(count // P...  32.4 us
    pallas_call x1, Pallas kernels, prologue(): pl.pallas_call(prologue_kernel, grid_spec=pltpu.PrefetchScalarGridSpec(nu...  10.1 us
    all_to_all x1, starting transfers between devices, body(): lax.all_to_all(jnp.broadcast_to(total[None], pieces.shape), ('dp', 'ctx')...  9.79 us
    all_to_all x1, starting transfers between devices, body(): lax.all_to_all(weight_part.reshape(devices, SLOT, MAIN), ('dp', 'ctx'), 0...  9.51 us
    all_to_all x1, starting transfers between devices, body(): arrived = lax.all_to_all(packed, 'ctx', 0, 0, tiled=True)  9.29 us
    all_to_all x1, starting transfers between devices, body(): back = lax.all_to_all(far_out, 'ctx', 0, 0, tiled=True)  7.22 us
    pallas_call x1, Pallas kernels, project(): pl.pallas_call(output_kernel, grid_spec=pltpu.PrefetchScalarGridSpec(num_...  7.01 us
  transfers between devices with their start and end apart: 4, of which 0 were waited for; matrix products, arithmetic and copies ran while one was open for 0% of the time, Pallas kernels for 55%

profile of v5, /device:TPU:1, one launch (start us, length us, event | category | flops | bytes accessed | tf_op | source)
XLA Modules:
  0.0 139.5 jit_solution(11910264550350294870)
XLA Ops:
  0.6 10.1 %prologue.1 = (bf16[16,192,1024]{2,1,0:T(8,128)(2,1)}, bf16[16,64,1024]{2,1,0:T(8,128)(2,1)}, bf16[16,64,256]{2,1,0:T(8,128)(2,1)}, f32[2,8,128]{2,1,0:T(8,128)}) custom-call(s32[16]{0:T(128)} %off_ref.7, bf16[1024,768]{1,0:T(8,128)(2,1)} %bitcast.16, bf16[1024,768]{1,0:T(8,128)(2,1)} %bitcast.17, bf16[1024,768]{1,0:T(8,128)(2,1)} %bitcast.18, ...), custom_call_target="tpu_custom_call" | custom-call | flops 2147483648 | bytes 14680064 | tf_op jit(solution)/shard_map/prologue/pallas_call | solution.py:293
  10.7 9.3 %all-to-all-start = ((bf16[16,64,256]{2,1,0:T(8,128)(2,1)}), bf16[16,64,256]{2,1,0:T(8,128)(2,1)S(1)}, u32[]{:S(2)}, u32[]{:S(2)}) async-start(bf16[16,64,256]{2,1,0:T(8,128)(2,1)} %get-tuple-element.28), calls=%async_computation | async-start | bytes 1048576 | tf_op jit(solution)/shard_map/all_to_all | solution.py:438
  20.0 16.1 %near_forward.2 = (bf16[8,1024,1024]{2,1,0:T(8,128)(2,1)}, bf16[768,1024]{1,0:T(8,128)(2,1)}, f32[8,8,1024]{2,1,0:T(8,128)}) custom-call(bf16[16,192,1024]{2,1,0:T(8,128)(2,1)} %get-tuple-element.23.stack_ref, f32[2,8,128]{2,1,0:T(8,128)} %get-tuple-element.24.bound_ref), custom_call_target="tpu_custom_call" | custom-call | flops 8589934592 | bytes 16777216 | tf_op jit(solution)/shard_map/near_forward/pallas_call | solution.py:325
  36.1 0.0 all-to-all-done
  36.1 4.9 %far.1 = bf16[1024,256]{1,0:T(8,128)(2,1)} custom-call(bf16[1024,256]{1,0:T(8,128)(2,1)S(1)} %bitcast.13), custom_call_target="tpu_custom_call" | custom-call | flops 3221225472 | bytes 1048576 | tf_op jit(solution)/shard_map/far/pallas_call | solution.py:350
  41.0 7.2 %all-to-all-start.1 = ((bf16[16,64,256]{2,1,0:T(8,128)(2,1)}), bf16[16,64,256]{2,1,0:T(8,128)(2,1)S(1)}, u32[]{:S(2)}, u32[]{:S(2)}) async-start(bf16[16,64,256]{2,1,0:T(8,128)(2,1)} %bitcast.5), calls=%async_computation.1 | async-start | bytes 1048576 | tf_op jit(solution)/shard_map/all_to_all | solution.py:442
  48.2 0.0 copy-start.1
  48.2 0.0 copy-start.2
  48.2 0.0 copy-start.3
  48.3 16.3 %near_forward.3 = (bf16[8,1024,1024]{2,1,0:T(8,128)(2,1)}, bf16[768,1024]{1,0:T(8,128)(2,1)}, f32[8,8,1024]{2,1,0:T(8,128)}) custom-call(bf16[16,192,1024]{2,1,0:T(8,128)(2,1)} %get-tuple-element.23.stack_ref, f32[2,8,128]{2,1,0:T(8,128)} %get-tuple-element.24.bound_ref, bf16[768,1024]{1,0:T(8,128)(2,1)} %get-tuple-element.25.refs_0_), custom_call_target="tpu_custom_call", output_to_operand_aliasing={{1}: (2, {})} | custom-call | flops 8589934592 | bytes 16777216 | tf_op jit(solution)/shard_map/near_forward/pallas_call | solution.py:325
  64.5 0.0 all-to-all-done.1.back_ref
  64.5 0.0 copy-start
  64.5 0.0 copy-done.1
  64.6 0.0 copy-done.2
  64.6 0.0 copy-done.3
  64.6 0.0 copy-start.4
  64.6 1.6 %copy-done.4 = bf16[768,1024]{1,0:T(8,128)(2,1)S(1)} copy-done((bf16[768,1024]{1,0:T(8,128)(2,1)S(1)}, bf16[768,1024]{1,0:T(8,128)(2,1)}, u32[]{:S(2)}) %copy-start.4) | copy-done | bytes 1572888
  66.2 7.0 %project.1 = (bf16[1024,768]{1,0:T(8,128)(2,1)}, bf16[2,64,8,640]{3,2,1,0:T(8,128)(2,1)}) custom-call(s32[16]{0:T(128)S(1)} %copy-done.3, bf16[768,1024]{1,0:T(8,128)(2,1)S(1)} %copy-done.4, bf16[16,64,1024]{2,1,0:T(8,128)(2,1)} %get-tuple-element.27.sel_ref, bf16[16,64,256]{2,1,0:T(8,128)(2,1)S(1)} %all-to-all-done.1.back_ref, ...), custom_call_target="tpu_custom_call" | custom-call | flops 2415919104 | bytes 10485760 | tf_op jit(solution)/shard_map/project/pallas_call | solution.py:363
  73.2 0.0 copy-done
  73.2 9.5 %all-to-all-start.2 = ((bf16[128,8,640]{2,1,0:T(8,128)(2,1)}), bf16[128,8,640]{2,1,0:T(8,128)(2,1)S(1)}, u32[]{:S(2)}, u32[]{:S(2)}) async-start(bf16[128,8,640]{2,1,0:T(8,128)(2,1)} %bitcast.10), calls=%async_computation.2 | async-start | bytes 2621440 | tf_op jit(solution)/shard_map/all_to_all | solution.py:446
  82.7 22.0 %near_backward.2 = (bf16[1024,768]{1,0:T(8,128)(2,1)}, bf16[1024,768]{1,0:T(8,128)(2,1)}, bf16[1024,768]{1,0:T(8,128)(2,1)}) custom-call(s32[16]{0:T(128)} %off_ref.7, bf16[8,1024,1024]{2,1,0:T(8,128)(2,1)} %get-tuple-element.32.e_ref, bf16[16,192,1024]{2,1,0:T(8,128)(2,1)} %get-tuple-element.23.stack_ref, bf16[16,64,1024]{2,1,0:T(8,128)(2,1)} %get-tuple-element.27.sel_ref, ...), custom_call_target="tpu_custom_call" | custom-call | flops 17179869184 | bytes 16777216 | tf_op jit(solution)/shard_map/near_backward/pallas_call | solution.py:410
  104.7 0.0 all-to-all-done.2
  104.7 0.2 reduce_sum.12
  104.9 1.2 broadcast_in_dim.22
  106.1 9.8 %all-to-all-start.3 = ((bf16[128,8,640]{2,1,0:T(8,128)(2,1)}), bf16[128,8,640]{2,1,0:T(8,128)(2,1)S(1)}, u32[]{:S(2)}, u32[]{:S(2)}) async-start(bf16[128,8,640]{2,1,0:T(8,128)(2,1)} %broadcast_in_dim.22), calls=%async_computation.3 | async-start | bytes 2621440 | tf_op jit(solution)/shard_map/all_to_all | solution.py:449
  115.9 22.0 %near_backward.3 = (bf16[1024,768]{1,0:T(8,128)(2,1)}, bf16[1024,768]{1,0:T(8,128)(2,1)}, bf16[1024,768]{1,0:T(8,128)(2,1)}) custom-call(s32[16]{0:T(128)} %off_ref.7, bf16[8,1024,1024]{2,1,0:T(8,128)(2,1)} %get-tuple-element.30.e_ref, ...), custom_call_target="tpu_custom_call", output_to_operand_aliasing={{0}: (7, {}), {1}: (8, {}), {2}: (9, {})} | custom-call | flops 17179869184 | bytes 16777216 | tf_op jit(solution)/shard_map/near_backward/pallas_call | solution.py:410
  138.0 0.0 all-to-all-done.3
  138.0 1.5 %unpack.1 = f32[768,768]{1,0:T(8,128)} custom-call(bf16[2,64,8,640]{3,2,1,0:T(8,128)(2,1)S(1)} %bitcast.12), custom_call_target="tpu_custom_call" | custom-call | flops 589824 | bytes 4194304 | tf_op jit(solution)/shard_map/unpack/pallas_call | solution.py:393
Async XLA Ops:
  10.7 25.4 %all-to-all-start = ((bf16[16,64,256]{2,1,0:T(8,128)(2,1)}), bf16[16,64,256]{2,1,0:T(8,128)(2,1)S(1)}, u32[]{:S(2)}, u32[]{:S(2)}) async-start(bf16[16,64,256]{2,1,0:T(8,128)(2,1)} %get-tuple-element.28), calls=%async_computation | async-start | bytes 1048576 | tf_op jit(solution)/shard_map/all_to_all | solution.py:438
  41.0 23.5 %all-to-all-start.1 = ((bf16[16,64,256]{2,1,0:T(8,128)(2,1)}), bf16[16,64,256]{2,1,0:T(8,128)(2,1)S(1)}, u32[]{:S(2)}, u32[]{:S(2)}) async-start(bf16[16,64,256]{2,1,0:T(8,128)(2,1)} %bitcast.5), calls=%async_computation.1 | async-start | bytes 1048576 | tf_op jit(solution)/shard_map/all_to_all | solution.py:442
  48.2 16.3 %copy-start.1 = (bf16[1,1024,768]{2,1,0:T(8,128)(2,1)S(1)}, bf16[1,1024,768]{2,1,0:T(8,128)(2,1)}, u32[]{:S(2)}) copy-start(bf16[1,1024,768]{2,1,0:T(8,128)(2,1)} %param.11) | copy-start | bytes 4718596
  48.2 16.3 %copy-start.2 = (bf16[768,768]{1,0:T(8,128)(2,1)S(1)}, bf16[768,768]{1,0:T(8,128)(2,1)}, u32[]{:S(2)}) copy-start(bf16[768,768]{1,0:T(8,128)(2,1)} %w_ref.3) | copy-start | bytes 3538948
  48.2 16.3 %copy-start.3 = (s32[16]{0:T(128)S(1)}, s32[16]{0:T(128)}, u32[]{:S(2)}) copy-start(s32[16]{0:T(128)} %off_ref.7) | copy-start | bytes 196
  64.5 8.6 %copy-start = (bf16[16,64,256]{2,1,0:T(8,128)(2,1)}, bf16[16,64,256]{2,1,0:T(8,128)(2,1)S(1)}, u32[]{:S(2)}) copy-start(bf16[16,64,256]{2,1,0:T(8,128)(2,1)S(1)} %all-to-all-done.1.back_ref) | copy-start | bytes 1572868
  64.6 1.6 %copy-start.4 = (bf16[768,1024]{1,0:T(8,128)(2,1)S(1)}, bf16[768,1024]{1,0:T(8,128)(2,1)}, u32[]{:S(2)}) copy-start(bf16[768,1024]{1,0:T(8,128)(2,1)} %get-tuple-element.26.att_ref) | copy-start | bytes 4718596
  73.2 31.5 %all-to-all-start.2 = ((bf16[128,8,640]{2,1,0:T(8,128)(2,1)}), bf16[128,8,640]{2,1,0:T(8,128)(2,1)S(1)}, u32[]{:S(2)}, u32[]{:S(2)}) async-start(bf16[128,8,640]{2,1,0:T(8,128)(2,1)} %bitcast.10), calls=%async_computation.2 | async-start | bytes 2621440 | tf_op jit(solution)/shard_map/all_to_all | solution.py:446
  106.1 31.8 %all-to-all-start.3 = ((bf16[128,8,640]{2,1,0:T(8,128)(2,1)}), bf16[128,8,640]{2,1,0:T(8,128)(2,1)S(1)}, u32[]{:S(2)}, u32[]{:S(2)}) async-start(bf16[128,8,640]{2,1,0:T(8,128)(2,1)} %broadcast_in_dim.22), calls=%async_computation.3 | async-start | bytes 2621440 | tf_op jit(solution)/shard_map/all_to_all | solution.py:449
